TPU v7x, 512 devices: a whole 4x8x8 slice. The times are simulated.
512 devices in a mesh: terms: 128 (over y, z_hi, x), rows: 4 (over z_lo, core).
Axes of the slice: x: 4, y: 8, z: 8 (z_hi: 4, z_lo: 2; z = z_hi * 2 + z_lo), core: 2. Of those that a mesh axis runs over, the one named last changes fastest.
Arguments:
- psi: float32 [2, 768, 768], P(None, 'rows'), may hold values from -6 to 6
- left_ops: float32 [128, 768, 768], P('terms', 'rows'), may hold values from -0.21875 to 0.21875
- right_ops: float32 [256, 768, 768], P('terms', 'rows'), may hold values from -0.0625 to 0.0625
- term_count: int32 [128], P('terms'), may hold values from 1 to 3, 192 in all
- right_slot: int32 [384], P('terms'), may hold values from 0 to 1
- sector: int32 [384], P('terms'), may hold values from 0 to 1
- sign_bit: int32 [384], P('terms'), may hold values from 0 to 1
Outputs:
- sigma: float32 [2, 768, 768], P(None, 'rows', 'terms')
Inputs may be any that keep to these rules, and one draw needn't show every extreme that they name: Owner o's live terms are its first term_count[o] slots of 3; right_slot, sector and sign_bit of the other slots have no effect.
All inputs are finite; a program needn't handle non-finite values. No bound on the sum of `term_count` on one device may be relied on, other than what follows from the above.
Results may differ from a plain program's by a relative error of at most 0.0003.
Values sent between devices are 32-bit elements; how exact they have to be, the bound alone decides.
No kernel may reach another device: no remote copies, remote signals or barrier semaphores. Data moves between devices by JAX's collectives and lax.ppermute only.
A program may use at most 64 MiB of HBM per device.

v0:
```python
import jax
import jax.numpy as jnp
from jax import lax
from jax.sharding import Mesh
from jax.sharding import PartitionSpec as P

TERMS = ("terms_0", "terms_1", "terms_2")


highest_mode = lax.Precision.HIGHEST


def passed_along(block, axis, distance):
    devices = range(lax.axis_size(axis))
    route = [((i - distance) % len(devices), i) for i in devices]
    return lax.ppermute(block, axis, route)


def in_blocks(shard, dim, length):
    before, after = (shard.shape[:dim], shard.shape[dim + 1 :])
    return jnp.moveaxis(shard.reshape(*before, length, -1, *after), dim, 0)


def summed_on_arrival(shard, axis, dim):
    tiles = in_blocks(shard, dim, lax.axis_size(axis))
    arrived = lax.all_to_all(tiles, axis, split_axis=0, concat_axis=0, tiled=True)
    return arrived.sum(axis=0)


def summed_rows(shard, axes, dim):
    far, near = axes
    own = summed_on_arrival(in_blocks(shard, dim, lax.axis_size(far)), near, dim + 1)
    return jnp.sum(lax.all_to_all(own, far, 0, 0, tiled=True), axis=0)


def per_device(psi, left_ops, right_ops, term_count, right_slot, sector, sign_bit):
    slot_count = right_slot.shape[0]
    rights_here = right_ops.shape[0]
    sector_count = psi.shape[0]
    live_count = term_count[0]
    is_live = lax.iota(jnp.int32, slot_count) < live_count
    term_weight = jnp.where(is_live, 2.0 * sign_bit.astype(jnp.float32) - 1.0, 0.0)
    left_rows = left_ops[0]
    inner_rows = jnp.einsum(
        "an,snb->sab",
        left_rows,
        lax.all_gather(psi, "rows", axis=1, tiled=True),
        precision=highest_mode,
    )
    sector_hit = (sector[None, :] == lax.iota(jnp.int32, sector_count)[:, None]).astype(
        jnp.float32
    ) * term_weight[None, :]
    slot_hit = (right_slot[:, None] == lax.iota(jnp.int32, rights_here)[None, :]).astype(
        jnp.float32
    )
    mixing = jnp.dot(sector_hit, slot_hit, precision=highest_mode)
    half_axis = lax.axis_size(TERMS) // 2
    moved_right = passed_along(right_ops, TERMS, half_axis)
    combined = jnp.einsum(
        "sr,rnb->snb",
        mixing,
        lax.all_gather(moved_right, "rows", axis=1, tiled=True),
        precision=highest_mode,
    )
    partial_value = jnp.einsum("sab,snb->san", inner_rows, combined, precision=highest_mode)
    return summed_rows(partial_value, (("terms_0", "terms_1"), "terms_2"), 2)


def solution(mesh):
    finer = Mesh(
        mesh.devices.reshape(8, 4, 4, mesh.shape["rows"]), ("terms_0", "terms_1", "terms_2", "rows")
    )
    placed = (
        P(None, "rows", None),
        P(TERMS, "rows", None),
        P(TERMS, "rows", None),
        P(TERMS),
        P(TERMS),
        P(TERMS),
        P(TERMS),
    )
    return jax.shard_map(
        per_device, mesh=finer, in_specs=placed, out_specs=P(None, "rows", TERMS), check_vma=False
    )
```

profile of v0, /device:TPU:8, one launch (start us, length us, event | category | flops | bytes accessed | tf_op | source)
XLA Modules:
  0.0 216.5 jit_solution(18297709809991915727)
XLA Ops:
  6.5 0.0 copy-start
  6.5 0.0 copy-start.2
  6.5 0.0 copy-start.3
  6.5 0.0 copy-start.4
  6.5 0.0 all-gather.3.cloned.1.call-start
  6.6 0.7 all-gather.3.cloned.1.call-update
  7.3 0.0 all-gather.5.cloned.1.call-start
  7.3 2.2 %copy.17 = f32[2,192,768]{2,0,1:T(2,128)S(1)} copy(f32[2,192,768]{2,1,0:T(8,128)} %param.9) | data formatting | bytes 2359296 | tf_op args[2]
  9.5 6.8 %collective-permute-start = (f32[2,192,768]{2,0,1:T(2,128)S(1)}, f32[2,192,768]{2,0,1:T(2,128)S(1)}, u32[]{:S(2)}, u32[]{:S(2)}) collective-permute-start(f32[2,192,768]{2,0,1:T(2,128)S(1)} %copy.17), channel_id=1, source_target_pairs={{256,0},{260,4},{264,8},{268,12},{272,16},{276,20},{280,24},{284,2... | collective-permute-start | bytes 3538952 | tf_op jit(solution)/shard_map/ppermute | solution.py:16
  16.3 51.9 %collective-permute-done = f32[2,192,768]{2,0,1:T(2,128)S(1)} collective-permute-done((f32[2,192,768]{2,0,1:T(2,128)S(1)}, f32[2,192,768]{2,0,1:T(2,128)S(1)}, u32[]{:S(2)}, u32[]{:S(2)}) %collective-permute-start) | collective-permute-done | bytes 1179680 | tf_op jit(solution)/shard_map/ppermute | solution.py:16
  68.3 0.0 copy-start.1
  68.3 1.0 copy-done.1
  69.3 0.0 all-gather.5.cloned.1.call-update
  70.0 0.0 copy-done.2
  70.0 0.0 copy-done.3
  70.0 0.0 copy-done.4
  70.0 0.2 convolution_bitcast_fusion
  70.2 0.0 all-gather.3.cloned.1.call-done
  70.2 0.0 copy-done
  70.2 5.5 %fusion.2 = f32[2,768,192]{1,2,0:T(8,128)S(1)} fusion(f32[2,768,768]{2,1,0:T(8,128)} %all-gather.3.cloned.1.call-done, f32[1,192,768]{2,1,0:T(8,128)S(1)} %copy-done), kind=kOutput, calls=%fused_computation.3 | convolution fusion | flops 2717908992 | bytes 6488064 | tf_op jit(solution)/shard_map/an,snb->sab/dot_general | solution.py:44
  75.8 54.2 %all-gather.5.cloned.1.call-done = f32[2,768,768]{2,0,1:T(2,128)} async-done(((f32[2,192,768]{2,0,1:T(2,128)}), f32[2,768,768]{2,0,1:T(2,128)}) %all-gather.5.cloned.1.call-update) | async-done | bytes 4718608 | tf_op jit(solution)/shard_map/all_gather | solution.py:62
  130.0 18.7 %fusion.10 = f32[2,768,768]{2,0,1:T(2,128)S(1)} fusion(f32[2,2,1]{1,0,2:T(2,128)S(1)} %convolution_bitcast_fusion, f32[2,768,768]{2,0,1:T(2,128)} %all-gather.5.cloned.1.call-done), kind=kOutput, calls=%fused_computation.14 | convolution fusion | flops 28311552 | bytes 9437200 | tf_op jit(solution)/shard_map/sr,rnb->snb/dot_general | solution.py:59
  148.7 4.1 %fusion = f32[2,192,768]{1,2,0:T(8,128)S(1)} fusion(f32[2,768,192]{1,2,0:T(8,128)S(1)} %fusion.2, f32[2,768,768]{2,0,1:T(2,128)S(1)} %fusion.10), kind=kOutput, calls=%fused_computation | convolution fusion | flops 2717908992 | bytes 7077888 | tf_op jit(solution)/shard_map/sab,snb->san/dot_general | solution.py:65
  152.8 0.5 copy.20
  153.3 0.2 copy.21
  153.5 26.0 %all_to_all.10 = f32[4,32,2,192,6]{3,1,4,2,0:T(8,128)S(1)} all-to-all(f32[4,32,2,192,6]{3,1,4,2,0:T(8,128)S(1)} %copy.21), channel_id=1, replica_groups=mesh['terms_0'=8,'terms_1'=4,'terms_2'=4,'rows'=4] {'terms_2'}, dimensions={0} | all-to-all | bytes 2359296 | tf_op jit(solution)/shard_map/all_to_all | solution.py:26
  179.4 0.2 reduce_sum.18
  179.6 0.3 copy.23
  179.9 29.0 %all_to_all.11 = f32[32,2,192,6]{2,1,3,0:T(2,128)S(1)} all-to-all(f32[32,2,192,6]{2,1,3,0:T(2,128)S(1)} %copy.23), channel_id=1, replica_groups=mesh['terms_0'=8,'terms_1'=4,'terms_2'=4,'rows'=4] {'terms_0','terms_1'}, dimensions={0} | all-to-all | bytes 589824 | tf_op jit(solution)/shard_map/all_to_all | solution.py:33
  208.9 0.8 reduce_sum.19
  (1 shorter events, 0.0 us)
Async XLA Ops:
  6.5 63.7 %copy-start = (f32[1,192,768]{2,1,0:T(8,128)S(1)}, f32[1,192,768]{2,1,0:T(8,128)}, u32[]{:S(2)}) copy-start(f32[1,192,768]{2,1,0:T(8,128)} %param.8) | copy-start | bytes 1769476
  6.5 63.5 %copy-start.2 = (s32[3]{0:T(128)S(1)}, s32[3]{0:T(128)}, u32[]{:S(2)}) copy-start(s32[3]{0:T(128)} %param.13) | copy-start | bytes 40
  6.5 63.5 %copy-start.3 = (s32[3]{0:T(128)S(1)}, s32[3]{0:T(128)}, u32[]{:S(2)}) copy-start(s32[3]{0:T(128)} %param.11) | copy-start | bytes 40
  6.5 63.5 %copy-start.4 = (s32[3]{0:T(128)S(1)}, s32[3]{0:T(128)}, u32[]{:S(2)}) copy-start(s32[3]{0:T(128)} %param.12) | copy-start | bytes 40
  6.5 63.7 %all-gather.3.cloned.1.call-start = ((), (), s32[]{:S(2)}) async-start(), calls=%async_computation.2 | async-start | bytes 5898240 | tf_op jit(solution)/shard_map/all_gather | solution.py:47
  7.3 122.7 %all-gather.5.cloned.1.call-start = ((), (), s32[]{:S(2)}) async-start(), calls=%async_computation.3 | async-start | bytes 5898240 | tf_op jit(solution)/shard_map/all_gather | solution.py:62
  9.5 58.8 %collective-permute-start = (f32[2,192,768]{2,0,1:T(2,128)S(1)}, f32[2,192,768]{2,0,1:T(2,128)S(1)}, u32[]{:S(2)}, u32[]{:S(2)}) collective-permute-start(f32[2,192,768]{2,0,1:T(2,128)S(1)} %copy.17), channel_id=1, source_target_pairs={{256,0},{260,4},{264,8},{268,12},{272,16},{276,20},{280,24},{284,2... | collective-permute-start | bytes 3538952 | tf_op jit(solution)/shard_map/ppermute | solution.py:16
  68.3 1.0 copy-start.1
Sparse Core Ops, SparseCore 0:
  9.4 60.1 all-gather.2
  71.7 58.2 all-gather.4
where the time goes:
time: 217 us
  waiting for transfers between devices  107 us (49%)
  blocking collectives  55 us (25%)
  matrix products  28.6 us (13%)
  between operations  14.2 us (7%)
  starting transfers between devices  6.9 us (3%)
  local copies, waits for them, and re-layouts  4.16 us (2%)
    all_gather x1, waiting for transfers between devices, per_device(): lax.all_gather(moved_right, 'rows', axis=1, tiled=True)  54.2 us
    ppermute x1, waiting for transfers between devices, passed_along(): return lax.ppermute(block, axis, route)  51.9 us
    all_to_all x1, blocking collectives, summed_rows(): return jnp.sum(lax.all_to_all(own, far, 0, 0, tiled=True), axis=0)  29 us
    all_to_all x1, blocking collectives, summed_on_arrival(): lax.all_to_all(tiles, axis, split_axis=0, concat_axis=0, tiled=True)  26 us
    dot_general x1, matrix products, per_device(): jnp.einsum('sr,rnb->snb', mixing, lax.all_gather(moved_right, 'rows', axi...  18.7 us
    ppermute x1, starting transfers between devices, passed_along(): return lax.ppermute(block, axis, route)  6.83 us
    dot_general x1, matrix products, per_device(): jnp.einsum('an,snb->sab', left_rows, lax.all_gather(psi, 'rows', axis=1,...  5.55 us
  transfers between devices with their start and end apart: 3, of which 2 were waited for; matrix products, arithmetic and copies ran while one was open for 4% of the time, Pallas kernels for 0%

commit v1 on v0

v1 whole, which is shorter than its diff:
```python
import jax
import jax.numpy as jnp
from jax import lax
from jax.sharding import Mesh
from jax.sharding import PartitionSpec as P

FINE = ("yh", "yl", "zh", "x", "zl", "c")
SIZES = (4, 2, 4, 4, 2, 2)
TERMS = FINE[:4]
ROWS = FINE[4:]


def shifted(block, axis, distance):
    n = lax.axis_size(axis)
    return lax.ppermute(block, axis, [(i, (i + distance) % n) for i in range(n)])


def from_next_pair(block):
    n = lax.axis_size(("zh", "zl"))
    return lax.ppermute(block, ("zh", "zl"), [(z, (z + (1 if z % 2 else -1)) % n) for z in range(n)])


def by_place(blocks, dim):
    shape = blocks.shape
    pairs = blocks.reshape(*shape[:dim], 2, 2, *shape[dim + 1 :])
    pairs = jnp.where(lax.axis_index("zl") == 1, jnp.flip(pairs, dim), pairs)
    pairs = jnp.where(lax.axis_index("c") == 1, jnp.flip(pairs, dim + 1), pairs)
    return pairs.reshape(shape)


def per_device(psi, left_ops, right_ops, term_count, right_slot, sector, sign_bit):
    sectors, rows, m = psi.shape
    rights = right_ops.shape[0]
    left = shifted(left_ops[0], "yh", 2)
    right_z = shifted(right_ops, "zl", 1)
    psi_z = from_next_pair(psi)
    psi_c = shifted(psi, "c", 1)
    right_c = shifted(right_ops, "c", 1)

    is_live = lax.iota(jnp.int32, right_slot.shape[0]) < term_count[0]
    weight = jnp.where(is_live, 2.0 * sign_bit.astype(jnp.float32) - 1.0, 0.0)
    in_sector = sector[None, :] == lax.iota(jnp.int32, sectors)[:, None]
    in_slot = right_slot[None, :] == lax.iota(jnp.int32, rights)[:, None]
    hit = in_sector[:, None, :] & in_slot[None, :, :]
    mixing = shifted(jnp.sum(jnp.where(hit, weight, 0.0), axis=-1), "yh", 2)

    psi_zc = shifted(psi_z, "c", 1)
    right_zc = shifted(right_z, "c", 1)

    left_x = by_place(left.reshape(rows, 4, rows), 1).reshape(rows, m)
    psi_x = jnp.concatenate([psi, psi_c, psi_z, psi_zc], axis=1)
    inner = jnp.einsum("an,snc->sac", left_x, psi_x, precision=lax.Precision.HIGH)
    right_x = jnp.concatenate([right_ops, right_c, right_z, right_zc], axis=1)
    combined = sum(mixing[:, r, None, None] * right_x[r][None] for r in range(rights))
    part = jnp.einsum("sdc,sac->dsa", combined, inner, precision=lax.Precision.HIGH)

    tall = part.reshape(4, 2, 4, 4, -1, sectors * rows).transpose(3, 1, 0, 2, 4, 5)
    tall = tall.reshape(8, -1, sectors * rows)
    got = lax.all_to_all(tall, ("x", "yl"), 0, 0, tiled=True).sum(axis=0)
    small = by_place(got.reshape(4, 4, -1, sectors * rows), 0)
    small = small.reshape(16, -1, sectors * rows)
    own = lax.all_to_all(small, ("yh", "zh"), 0, 0, tiled=True).sum(axis=0)
    return own.reshape(-1, sectors, rows).transpose(1, 2, 0)


def solution(mesh):
    finer = Mesh(mesh.devices.reshape(SIZES), FINE)
    placed = (
        P(None, ROWS, None),
        P(TERMS, ROWS, None),
        P(TERMS, ROWS, None),
        P(TERMS),
        P(TERMS),
        P(TERMS),
        P(TERMS),
    )
    return jax.shard_map(
        per_device, mesh=finer, in_specs=placed, out_specs=P(None, ROWS, TERMS), check_vma=False
    )
```

time: 217 us -> 122 us (0.56)
  the two profiles are of different devices: /device:TPU:8 before, /device:TPU:64 now
where the time goes in v1:
time: 122 us
  blocking collectives  50.6 us (41%)
  starting transfers between devices  32.2 us (26%)
  local copies, waits for them, and re-layouts  19.6 us (16%)
  waiting for transfers between devices  9.58 us (8%)
  matrix products  6.31 us (5%)
  other arithmetic  2.51 us (2%)
    ppermute x7, starting transfers between devices, shifted(): lax.ppermute(block, axis, [(i, (i + distance) % n) for i in range(n)])  30.2 us
    all_to_all x1, blocking collectives, per_device(): got = lax.all_to_all(tall, ('x', 'yl'), 0, 0, tiled=True).sum(axis=0)  25.8 us
    all_to_all x1, blocking collectives, per_device(): own = lax.all_to_all(small, ('yh', 'zh'), 0, 0, tiled=True).sum(axis=0)  24.9 us
    ppermute x7, waiting for transfers between devices, shifted(): lax.ppermute(block, axis, [(i, (i + distance) % n) for i in range(n)])  9.58 us
    unnamed x3, local copies, waits for them, and re-layouts  5.82 us
    dot_general x1, matrix products, per_device(): jnp.einsum('an,snc->sac', left_x, psi_x, precision=lax.Precision.HIGH)  3.6 us
    rev x1, local copies, waits for them, and re-layouts, by_place(): pairs = jnp.where(lax.axis_index('c') == 1, jnp.flip(pairs, dim + 1), pairs)  2.89 us
    dot_general x1, matrix products, per_device(): jnp.einsum('sdc,sac->dsa', combined, inner, precision=lax.Precision.HIGH)  2.72 us
  transfers between devices with their start and end apart: 8, of which 1 were waited for; matrix products, arithmetic and copies ran while one was open for 15% of the time, Pallas kernels for 0%

profile of v1, /device:TPU:64, one launch (start us, length us, event | category | flops | bytes accessed | tf_op | source)
XLA Modules:
  0.0 121.7 jit_solution(5634693965625655941)
XLA Ops:
  0.0 6.9 %collective-permute-start.6 = (f32[2,192,768]{2,1,0:T(8,128)}, f32[2,192,768]{2,1,0:T(8,128)S(1)}, u32[]{:S(2)}, u32[]{:S(2)}) collective-permute-start(f32[2,192,768]{2,1,0:T(8,128)} %param.9), channel_id=1, source_target_pairs={{0,2},{2,0},{1,3},{3,1},{4,6},{6,4},{5,7},{7,5},{8,10},{10,8},{9,1... | collective-permute-start | bytes 3538952 | tf_op jit(solution)/shard_map/ppermute | solution.py:15
  6.9 1.9 %collective-permute-start.1 = (f32[2,192,768]{2,1,0:T(8,128)}, f32[2,192,768]{2,1,0:T(8,128)}, u32[]{:S(2)}, u32[]{:S(2)}) collective-permute-start(f32[2,192,768]{2,1,0:T(8,128)} %param.7), channel_id=1, source_target_pairs={{0,50},{2,16},{16,2},{18,32},{32,18},{34,48},{48,34},{50,0},{1,51}... | collective-permute-start | bytes 3538952 | tf_op jit(solution)/shard_map/ppermute | solution.py:20
  8.8 1.9 %collective-permute-start.5 = (f32[2,192,768]{2,1,0:T(8,128)}, f32[2,192,768]{2,1,0:T(8,128)}, u32[]{:S(2)}, u32[]{:S(2)}) collective-permute-start(f32[2,192,768]{2,1,0:T(8,128)} %param.9), channel_id=1, source_target_pairs={{0,1},{1,0},{2,3},{3,2},{4,5},{5,4},{6,7},{7,6},{8,9},{9,8},{10,11... | collective-permute-start | bytes 3538952 | tf_op jit(solution)/shard_map/ppermute | solution.py:15
  10.8 7.5 %collective-permute-start.3 = (f32[192,768]{1,0:T(8,128)}, f32[192,768]{1,0:T(8,128)S(1)}, u32[]{:S(2)}, u32[]{:S(2)}) collective-permute-start(f32[192,768]{1,0:T(8,128)} %bitcast.16), channel_id=1, source_target_pairs={{0,256},{128,384},{256,0},{384,128},{1,257},{129,385},{257,1},{385... | collective-permute-start | bytes 1769480 | tf_op jit(solution)/shard_map/ppermute | solution.py:15
  18.2 0.7 iota_compare_fusion
  19.6 0.7 compare_select_fusion
  20.2 9.6 %collective-permute-done.6 = f32[2,192,768]{2,1,0:T(8,128)S(1)} collective-permute-done((f32[2,192,768]{2,1,0:T(8,128)}, f32[2,192,768]{2,1,0:T(8,128)S(1)}, u32[]{:S(2)}, u32[]{:S(2)}) %collective-permute-start.6) | collective-permute-done | bytes 1179680 | tf_op jit(solution)/shard_map/ppermute | solution.py:15
  29.8 1.9 %collective-permute-start.7 = (f32[2,192,768]{2,1,0:T(8,128)S(1)}, f32[2,192,768]{2,1,0:T(8,128)}, u32[]{:S(2)}, u32[]{:S(2)}) collective-permute-start(f32[2,192,768]{2,1,0:T(8,128)S(1)} %collective-permute-done.6), channel_id=1, source_target_pairs={{0,1},{1,0},{2,3},{3,2},{4,5},{5,4},{6,7},{7,6},{8,9},{9,8},{10,11... | collective-permute-start | bytes 3538952 | tf_op jit(solution)/shard_map/ppermute | solution.py:15
  31.7 0.1 fusion.19
  31.8 7.7 %collective-permute-start.4 = (f32[2,2]{1,0:T(2,128)S(1)}, f32[2,2]{1,0:T(2,128)S(1)}, u32[]{:S(2)}, u32[]{:S(2)}) collective-permute-start(f32[2,2]{1,0:T(2,128)S(1)} %fusion.19), channel_id=1, source_target_pairs={{0,256},{128,384},{256,0},{384,128},{1,257},{129,385},{257,1},{385... | collective-permute-start | bytes 56 | tf_op jit(solution)/shard_map/ppermute | solution.py:15
  39.5 2.4 %constant_dynamic-update-slice_fusion.3 = f32[2,768,768]{2,1,0:T(8,128)} fusion(f32[2,192,768]{2,1,0:T(8,128)} %param.9), kind=kLoop, calls=%fused_computation.26 | loop fusion | bytes 2359296
  41.9 0.0 collective-permute-done.4
  41.9 2.1 %collective-permute-start = (f32[2,192,768]{2,1,0:T(8,128)}, f32[2,192,768]{2,1,0:T(8,128)}, u32[]{:S(2)}, u32[]{:S(2)}) collective-permute-start(f32[2,192,768]{2,1,0:T(8,128)} %param.7), channel_id=1, source_target_pairs={{0,1},{1,0},{2,3},{3,2},{4,5},{5,4},{6,7},{7,6},{8,9},{9,8},{10,11... | collective-permute-start | bytes 3538952 | tf_op jit(solution)/shard_map/ppermute | solution.py:15
  44.0 0.2 slice_reduce_fusion.1
  44.2 0.0 collective-permute-done.3
  44.2 0.7 reshape_reshape.12
  45.0 0.0 collective-permute-done.1
  45.0 2.2 %collective-permute-start.2 = (f32[2,192,768]{2,1,0:T(8,128)}, f32[2,192,768]{2,1,0:T(8,128)}, u32[]{:S(2)}, u32[]{:S(2)}) collective-permute-start(f32[2,192,768]{2,1,0:T(8,128)} %collective-permute-done.1), channel_id=1, source_target_pairs={{0,1},{1,0},{2,3},{3,2},{4,5},{5,4},{6,7},{7,6},{8,9},{9,8},{10,11... | collective-permute-start | bytes 3538952 | tf_op jit(solution)/shard_map/ppermute | solution.py:15
  47.2 0.4 reverse_select_fusion
  47.6 2.9 %rev.17 = f32[192,2,2,192]{3,2,1,0:T(2,128)S(1)} reverse(f32[192,2,2,192]{3,2,1,0:T(2,128)S(1)} %reverse_select_fusion), dimensions={2} | reverse | bytes 1179648 | tf_op jit(solution)/shard_map/jit(_flip)/rev | solution.py:27
  50.5 0.5 broadcast_select_fusion
  51.1 0.8 reshape.52
  51.8 0.0 collective-permute-done.5
  51.8 2.4 %constant_dynamic-update-slice_fusion.2 = f32[2,768,768]{2,1,0:T(8,128)} fusion(f32[2,768,768]{2,1,0:T(8,128)} %constant_dynamic-update-slice_fusion.3, f32[2,192,768]{2,1,0:T(8,128)} %collective-permute-done.5), kind=kLoop, calls=%fused_computation.25 | loop fusion | bytes 2359296
  54.2 1.1 constant_dynamic-update-slice_fusion.1
  55.3 0.0 collective-permute-done.7
  55.3 2.4 %constant_dynamic-update-slice_fusion = f32[2,768,768]{2,1,0:T(8,128)} fusion(f32[2,768,768]{2,1,0:T(8,128)} %constant_dynamic-update-slice_fusion.1, f32[2,192,768]{2,1,0:T(8,128)} %collective-permute-done.7), kind=kLoop, calls=%fused_computation.23 | loop fusion | bytes 2359296 | tf_op jit(solution)/shard_map/concatenate | solution.py:53
  57.7 2.7 %slice_bitcast_fusion.1 = (f32[768,768]{1,0:T(8,128)S(1)}, f32[768,768]{1,0:T(8,128)S(1)}) fusion(f32[2,768,768]{2,1,0:T(8,128)} %constant_dynamic-update-slice_fusion), kind=kLoop, calls=%fused_computation.13 | loop fusion | bytes 9437184 | tf_op jit(solution)/shard_map/mul | solution.py:54
  60.3 0.0 collective-permute-done
  60.4 0.0 collective-permute-done.2
  60.4 3.6 %fusion = f32[2,768,192]{1,2,0:T(8,128)S(1)} fusion(f32[192,768,1]{1,0,2:T(8,128)S(1)} %reshape.52, f32[2,192,768]{2,1,0:T(8,128)} %collective-permute-done.2, f32[2,192,768]{2,1,0:T(8,128)} %collective-permute-done.1, f32[2,192,768]{2,1,0:T(8,128)} %collective-permute-done, f32[2,192,768]{2,1,0:T(8,128)} %param.7), kind=kOutput, calls=%fused_computation | convolution fusion | flops 1362493440 | bytes 6488064 | tf_op jit(solution)/shard_map/an,snc->sac/dot_general | solution.py:52
  64.0 2.7 %fusion.16 = f32[768,2,192]{0,2,1:T(8,128)S(1)} fusion(f32[2,768,192]{1,2,0:T(8,128)S(1)} %fusion, f32[768,768]{1,0:T(8,128)S(1)} %get-tuple-element.8, f32[2]{0:T(128)S(1)} %get-tuple-element.6, f32[768,768]{1,0:T(8,128)S(1)} %get-tuple-element.7, f32[2]{0:T(128)S(1)} %get-tuple-element.5), kind=kOutput, calls=%fused_computation.18 | convolution fusion | flops 1362493440 | bytes 7077904 | tf_op jit(solution)/shard_map/sdc,sac->dsa/dot_general | solution.py:55
  66.7 0.8 copy.16
  67.5 1.3 %reshape.49 = f32[4,2,4,4,6,384]{5,4,3,2,1,0:T(8,128)S(1)} reshape(f32[768,2,192]{2,1,0:T(2,128)S(1)} %copy.16) | data formatting | bytes 2359296 | tf_op jit(solution)/shard_map/reshape | solution.py:57
  68.8 0.2 copy.19
  69.0 1.2 reshape.54
  70.2 25.8 %all_to_all.10 = f32[8,96,384]{2,1,0:T(8,128)S(1)} all-to-all(f32[8,96,384]{2,1,0:T(8,128)} %reshape.54), channel_id=1, replica_groups=mesh['yh'=4,'yl'=2,'zh'=4,'x'=4,'zl'=2,'c'=2] {'x','yl'}, dimensions={0} | all-to-all | bytes 2359296 | tf_op jit(solution)/shard_map/all_to_all | solution.py:59
  96.0 0.1 reduce_sum.28
  96.1 24.9 %all_to_all.11 = f32[16,6,384]{2,1,0:T(8,128)S(1)} all-to-all(f32[16,6,384]{2,1,0:T(8,128)S(1)} %bitcast.15), channel_id=1, replica_groups=mesh['yh'=4,'yl'=2,'zh'=4,'x'=4,'zl'=2,'c'=2] {'yh','zh'}, dimensions={0} | all-to-all | bytes 294912 | tf_op jit(solution)/shard_map/all_to_all | solution.py:62
  121.0 0.7 reshape.51
  (4 shorter events, 0.1 us)
Async XLA Ops:
  0.0 29.8 %collective-permute-start.6 = (f32[2,192,768]{2,1,0:T(8,128)}, f32[2,192,768]{2,1,0:T(8,128)S(1)}, u32[]{:S(2)}, u32[]{:S(2)}) collective-permute-start(f32[2,192,768]{2,1,0:T(8,128)} %param.9), channel_id=1, source_target_pairs={{0,2},{2,0},{1,3},{3,1},{4,6},{6,4},{5,7},{7,5},{8,10},{10,8},{9,1... | collective-permute-start | bytes 3538952 | tf_op jit(solution)/shard_map/ppermute | solution.py:15
  6.9 38.1 %collective-permute-start.1 = (f32[2,192,768]{2,1,0:T(8,128)}, f32[2,192,768]{2,1,0:T(8,128)}, u32[]{:S(2)}, u32[]{:S(2)}) collective-permute-start(f32[2,192,768]{2,1,0:T(8,128)} %param.7), channel_id=1, source_target_pairs={{0,50},{2,16},{16,2},{18,32},{32,18},{34,48},{48,34},{50,0},{1,51}... | collective-permute-start | bytes 3538952 | tf_op jit(solution)/shard_map/ppermute | solution.py:20
  8.8 43.0 %collective-permute-start.5 = (f32[2,192,768]{2,1,0:T(8,128)}, f32[2,192,768]{2,1,0:T(8,128)}, u32[]{:S(2)}, u32[]{:S(2)}) collective-permute-start(f32[2,192,768]{2,1,0:T(8,128)} %param.9), channel_id=1, source_target_pairs={{0,1},{1,0},{2,3},{3,2},{4,5},{5,4},{6,7},{7,6},{8,9},{9,8},{10,11... | collective-permute-start | bytes 3538952 | tf_op jit(solution)/shard_map/ppermute | solution.py:15
  10.8 33.4 %collective-permute-start.3 = (f32[192,768]{1,0:T(8,128)}, f32[192,768]{1,0:T(8,128)S(1)}, u32[]{:S(2)}, u32[]{:S(2)}) collective-permute-start(f32[192,768]{1,0:T(8,128)} %bitcast.16), channel_id=1, source_target_pairs={{0,256},{128,384},{256,0},{384,128},{1,257},{129,385},{257,1},{385... | collective-permute-start | bytes 1769480 | tf_op jit(solution)/shard_map/ppermute | solution.py:15
  29.8 25.5 %collective-permute-start.7 = (f32[2,192,768]{2,1,0:T(8,128)S(1)}, f32[2,192,768]{2,1,0:T(8,128)}, u32[]{:S(2)}, u32[]{:S(2)}) collective-permute-start(f32[2,192,768]{2,1,0:T(8,128)S(1)} %collective-permute-done.6), channel_id=1, source_target_pairs={{0,1},{1,0},{2,3},{3,2},{4,5},{5,4},{6,7},{7,6},{8,9},{9,8},{10,11... | collective-permute-start | bytes 3538952 | tf_op jit(solution)/shard_map/ppermute | solution.py:15
  31.8 10.1 %collective-permute-start.4 = (f32[2,2]{1,0:T(2,128)S(1)}, f32[2,2]{1,0:T(2,128)S(1)}, u32[]{:S(2)}, u32[]{:S(2)}) collective-permute-start(f32[2,2]{1,0:T(2,128)S(1)} %fusion.19), channel_id=1, source_target_pairs={{0,256},{128,384},{256,0},{384,128},{1,257},{129,385},{257,1},{385... | collective-permute-start | bytes 56 | tf_op jit(solution)/shard_map/ppermute | solution.py:15
  41.9 18.4 %collective-permute-start = (f32[2,192,768]{2,1,0:T(8,128)}, f32[2,192,768]{2,1,0:T(8,128)}, u32[]{:S(2)}, u32[]{:S(2)}) collective-permute-start(f32[2,192,768]{2,1,0:T(8,128)} %param.7), channel_id=1, source_target_pairs={{0,1},{1,0},{2,3},{3,2},{4,5},{5,4},{6,7},{7,6},{8,9},{9,8},{10,11... | collective-permute-start | bytes 3538952 | tf_op jit(solution)/shard_map/ppermute | solution.py:15
  45.0 15.4 %collective-permute-start.2 = (f32[2,192,768]{2,1,0:T(8,128)}, f32[2,192,768]{2,1,0:T(8,128)}, u32[]{:S(2)}, u32[]{:S(2)}) collective-permute-start(f32[2,192,768]{2,1,0:T(8,128)} %collective-permute-done.1), channel_id=1, source_target_pairs={{0,1},{1,0},{2,3},{3,2},{4,5},{5,4},{6,7},{7,6},{8,9},{9,8},{10,11... | collective-permute-start | bytes 3538952 | tf_op jit(solution)/shard_map/ppermute | solution.py:15

commit v2 on v1

v2 whole, which is shorter than its diff:
```python
import jax
import jax.numpy as jnp
from jax import lax
from jax.experimental import pallas as pl
from jax.experimental.pallas import tpu as pltpu
from jax.sharding import Mesh
from jax.sharding import PartitionSpec as P


FINE = ("yh", "yl", "zh", "x", "zl", "c")
SIZES = (4, 2, 4, 4, 2, 2)
TERMS = FINE[:4]
ROWS = FINE[4:]
VMEM = pl.BlockSpec(memory_space=pltpu.VMEM)
SMEM = pl.BlockSpec(memory_space=pltpu.SMEM)
MIB = 1 << 20


def shifted(block, axis, distance):
    n = lax.axis_size(axis)
    return lax.ppermute(block, axis, [(i, (i + distance) % n) for i in range(n)])


def from_next_pair(block):
    n = lax.axis_size(("zh", "zl"))
    return lax.ppermute(
        block, ("zh", "zl"), [(z, (z + (1 if z % 2 else -1)) % n) for z in range(n)]
    )


def halves(value):
    high = value.astype(jnp.bfloat16)
    return high, (value - high.astype(jnp.float32)).astype(jnp.bfloat16)


def product(a, b, dims):
    return lax.dot_general(a, b, (dims, ((), ())), preferred_element_type=jnp.float32)


def three_pass(a, b, dims):
    return product(a[0], b[0], dims) + (product(a[0], b[1], dims) + product(a[1], b[0], dims))


def mixed(mix, block, s):
    return mix[s, 0] * block[0] + mix[s, 1] * block[1]


ROW = ((1,), (0,))
TURNED = ((1,), (1,))


def split_kernel(place, psi, psi_c, psi_h, psi_l):
    sectors, rows, _ = psi.shape
    for i, p in enumerate((psi, psi_c)):
        at = pl.ds(pl.multiple_of((place[1] ^ i) * rows, rows), rows)
        for s in range(sectors):
            psi_h[s, at, :], psi_l[s, at, :] = halves(p[s])


def mix_kernel(mix, right, right_c, comb_h, comb_l):
    for i, r in enumerate((right, right_c)):
        for s in range(comb_h.shape[1]):
            comb_h[i, s], comb_l[i, s] = halves(mixed(mix, r, s))


def near_kernel(place, left, psi_h, psi_l, near):
    half = psi_h.shape[1]
    mine = halves(left[:, pl.ds(pl.multiple_of(place[0] * half, 128), half)])
    for s in range(psi_h.shape[0]):
        near[s] = three_pass(mine, (psi_h[s], psi_l[s]), ROW)


def next_kernel(psi_z, next_h, next_l):
    for s in range(psi_z.shape[0]):
        next_h[s], next_l[s] = halves(psi_z[s])


def far_kernel(place, left, near, next_h, next_l, psi_zc, inner_h, inner_l):
    sectors, rows, half = psi_zc.shape[0], psi_zc.shape[1], left.shape[1] // 2
    other = left[:, pl.ds(pl.multiple_of((1 - place[0]) * half, 128), half)]
    swapped = jnp.concatenate([other[:, rows:], other[:, :rows]], axis=1)
    other = halves(jnp.where(place[1] == 1, swapped, other))
    for s in range(sectors):
        zc_h, zc_l = halves(psi_zc[s])
        far_h = jnp.concatenate([next_h[s], zc_h], axis=0)
        far_l = jnp.concatenate([next_l[s], zc_l], axis=0)
        inner = near[s] + three_pass(other, (far_h, far_l), ROW)
        inner_h[s], inner_l[s] = halves(inner)


def term_kernel(place, mix, inner_h, inner_l, comb_h, comb_l, right_z, right_zc, out, part, held, sem):
    sectors, _, _ = inner_h.shape
    mine = place[0] * 2 + place[1]
    fetch = pltpu.make_async_copy(right_z, held, sem)
    fetch.start()
    for i in range(4):
        if i == 2:
            fetch.wait()
        both = []
        for s in range(sectors):
            if i < 2:
                comb = comb_h[i, s], comb_l[i, s]
            else:
                comb = halves(mixed(mix, held if i == 2 else right_zc, s))
            both.append(three_pass(comb, (inner_h[s], inner_l[s]), TURNED))
        part[...] = jnp.concatenate(both, axis=1)
        for yl in range(2):
            for zh in range(4):
                for x in range(4):
                    at = yl * 96 + zh * 24 + x * 6
                    out[x * 2 + yl, mine ^ i, zh * 6 : zh * 6 + 6, :] = part[at : at + 6, :]


def call(kernel, shapes, specs, flops, scratch=()):
    step = pl.pallas_call(
        kernel,
        out_shape=shapes,
        in_specs=specs,
        out_specs=jax.tree.map(lambda _: VMEM, shapes),
        scratch_shapes=scratch,
        compiler_params=pltpu.CompilerParams(vmem_limit_bytes=24 * MIB),
        cost_estimate=pl.CostEstimate(flops=flops, bytes_accessed=8 * MIB, transcendentals=0),
    )
    return step


def per_device(psi, left_ops, right_ops, term_count, right_slot, sector, sign_bit):
    sectors, rows, m = psi.shape
    rights = right_ops.shape[0]
    f32, bf16 = jnp.float32, jnp.bfloat16
    shape = jax.ShapeDtypeStruct
    left = shifted(left_ops[0], "yh", 2)
    right_z = shifted(right_ops, "zl", 1)
    psi_z = from_next_pair(psi)
    psi_c = shifted(psi, "c", 1)
    right_c = shifted(right_ops, "c", 1)

    is_live = lax.iota(jnp.int32, right_slot.shape[0]) < term_count[0]
    weight = jnp.where(is_live, 2.0 * sign_bit.astype(f32) - 1.0, 0.0)
    in_sector = sector[None, :] == lax.iota(jnp.int32, sectors)[:, None]
    in_slot = right_slot[None, :] == lax.iota(jnp.int32, rights)[:, None]
    hit = in_sector[:, None, :] & in_slot[None, :, :]
    mixing = shifted(jnp.sum(jnp.where(hit, weight, 0.0), axis=-1), "yh", 2)

    psi_zc = shifted(psi_z, "c", 1)
    right_zc = shifted(right_z, "c", 1)

    place = jnp.stack([lax.axis_index("zl"), lax.axis_index("c")]).astype(jnp.int32)
    product_flops = 2 * sectors * rows * m * m
    prepared = shape((sectors, 2 * rows, m), bf16)
    combined = shape((2, sectors, rows, m), bf16)
    psi_h, psi_l = call(split_kernel, (prepared, prepared), [SMEM] + [VMEM] * 2, MIB)(
        place, psi, psi_c
    )
    comb_h, comb_l = call(mix_kernel, (combined, combined), [SMEM] + [VMEM] * 2, MIB)(
        mixing, right_ops, right_c
    )
    near = call(near_kernel, shape((sectors, rows, m), f32), [SMEM] + [VMEM] * 3, 3 * product_flops // 2)(
        place, left, psi_h, psi_l
    )
    inner = shape((sectors, rows, m), bf16)
    next_h, next_l = call(next_kernel, (inner, inner), [VMEM], MIB)(psi_z)
    inner_h, inner_l = call(
        far_kernel,
        (inner, inner),
        [SMEM] + [VMEM] * 5,
        3 * product_flops // 2,
    )(place, left, near, next_h, next_l, psi_zc)
    tall = call(
        term_kernel,
        shape((8, 4, 24, sectors * rows), f32),
        [SMEM, SMEM] + [VMEM] * 4 + [pl.BlockSpec(memory_space=pl.ANY), VMEM],
        3 * product_flops,
        [
            pltpu.VMEM((rows, sectors * rows), f32),
            pltpu.VMEM((rights, rows, m), f32),
            pltpu.SemaphoreType.DMA,
        ],
    )(place, mixing, inner_h, inner_l, comb_h, comb_l, right_z, right_zc)

    got = lax.all_to_all(tall.reshape(8, -1, sectors * rows), ("x", "yl"), 0, 0, tiled=True)
    small = got.sum(axis=0).reshape(16, -1, sectors * rows)
    own = lax.all_to_all(small, ("yh", "zh"), 0, 0, tiled=True).sum(axis=0)
    return own.reshape(-1, sectors, rows).transpose(1, 2, 0)


def solution(mesh):
    finer = Mesh(mesh.devices.reshape(SIZES), FINE)
    placed = (
        P(None, ROWS, None),
        P(TERMS, ROWS, None),
        P(TERMS, ROWS, None),
        P(TERMS),
        P(TERMS),
        P(TERMS),
        P(TERMS),
    )
    return jax.shard_map(
        per_device, mesh=finer, in_specs=placed, out_specs=P(None, ROWS, TERMS), check_vma=False
    )
```

time: 122 us -> 130 us (1.066)
  waiting for transfers between devices: 9.58 us -> 39.2 us
  local copies, waits for them, and re-layouts: 19.6 us -> 0.71 us
  Pallas kernels: 0 us -> 12.3 us
  blocking collectives: 50.6 us -> 43.8 us
  matrix products: 6.31 us -> 0 us
  starting transfers between devices: 32.2 us -> 30.7 us
    ppermute x7, waiting for transfers between devices: 9.58 us -> 25.5 us  [shifted(): lax.ppermute(block, axis, [(i, (i + distance) % n) for i in range(n)])]
    ppermute x1, waiting for transfers between devices: 0.01 us -> 13.7 us  [from_next_pair(): lax.ppermute(block, ('zh', 'zl'), [(z, (z + (1 if z % 2 else -1)) % n) fo...]
    pallas_call x0 -> x6, Pallas kernels: none -> 12.3 us  [the longest x1 3.93 us: per_device(): call(term_kernel, shape((8, 4, 24, sectors * rows), f32), [SMEM, SMEM] +...]
    dot_general x2 -> x0, matrix products: 6.31 us -> none  [the longest x1 3.6 us: per_device(): jnp.einsum('an,snc->sac', left_x, psi_x, precision=lax.Precision.HIGH)]
    unnamed x3 -> x4, local copies, waits for them, and re-layouts: 5.82 us -> 0.01 us
    ppermute x7, starting transfers between devices: 30.2 us -> 26.3 us  [shifted(): lax.ppermute(block, axis, [(i, (i + distance) % n) for i in range(n)])]
    all_to_all x1, blocking collectives: 24.9 us -> 21.2 us  [per_device(): own = lax.all_to_all(small, ('yh', 'zh'), 0, 0, tiled=True).sum(axis=0)]
    all_to_all x1, blocking collectives: 25.8 us -> 22.5 us  [per_device(): lax.all_to_all(tall.reshape(8, -1, sectors * rows), ('x', 'yl'), 0, 0, ti...]
  transfers between devices with their start and end apart: 8 -> 8, of which waited for: 1 -> 3; matrix products, arithmetic and copies ran while one was open for 15% -> 1% of each run, Pallas kernels for 0% -> 6%
where the time goes in v2:
time: 130 us; the launch traced here: 129 us
  blocking collectives  43.8 us (34%)
  waiting for transfers between devices  39.2 us (30%)
  starting transfers between devices  30.7 us (24%)
  Pallas kernels  12.3 us (9%)
  other arithmetic  1.6 us (1%)
    ppermute x7, starting transfers between devices, shifted(): lax.ppermute(block, axis, [(i, (i + distance) % n) for i in range(n)])  26.3 us
    ppermute x7, waiting for transfers between devices, shifted(): lax.ppermute(block, axis, [(i, (i + distance) % n) for i in range(n)])  25.5 us
    all_to_all x1, blocking collectives, per_device(): lax.all_to_all(tall.reshape(8, -1, sectors * rows), ('x', 'yl'), 0, 0, ti...  22.5 us
    all_to_all x1, blocking collectives, per_device(): own = lax.all_to_all(small, ('yh', 'zh'), 0, 0, tiled=True).sum(axis=0)  21.2 us
    ppermute x1, waiting for transfers between devices, from_next_pair(): lax.ppermute(block, ('zh', 'zl'), [(z, (z + (1 if z % 2 else -1)) % n) fo...  13.7 us
    ppermute x1, starting transfers between devices, from_next_pair(): lax.ppermute(block, ('zh', 'zl'), [(z, (z + (1 if z % 2 else -1)) % n) fo...  4.4 us
    pallas_call x1, Pallas kernels, per_device(): call(term_kernel, shape((8, 4, 24, sectors * rows), f32), [SMEM, SMEM] +...  3.93 us
  transfers between devices with their start and end apart: 8, of which 3 were waited for; matrix products, arithmetic and copies ran while one was open for 1% of the time, Pallas kernels for 6%

profile of v2, /device:TPU:64, one launch (start us, length us, event | category | flops | bytes accessed | tf_op | source)
XLA Modules:
  0.0 129.1 jit_solution(17651729648822328513)
XLA Ops:
  0.0 0.0 copy-start
  0.0 4.4 %collective-permute-start.3 = (f32[2,192,768]{2,1,0:T(8,128)}, f32[2,192,768]{2,1,0:T(8,128)}, u32[]{:S(2)}, u32[]{:S(2)}) collective-permute-start(f32[2,192,768]{2,1,0:T(8,128)} %psi.1), channel_id=1, source_target_pairs={{0,50},{2,16},{16,2},{18,32},{32,18},{34,48},{48,34},{50,0},{1,51}... | collective-permute-start | bytes 3538952 | tf_op jit(solution)/shard_map/ppermute | solution.py:26
  4.4 8.2 %collective-permute-start.6 = (f32[2,192,768]{2,1,0:T(8,128)}, f32[2,192,768]{2,1,0:T(8,128)}, u32[]{:S(2)}, u32[]{:S(2)}) collective-permute-start(f32[2,192,768]{2,1,0:T(8,128)} %right.1), channel_id=1, source_target_pairs={{0,2},{2,0},{1,3},{3,1},{4,6},{6,4},{5,7},{7,5},{8,10},{10,8},{9,1... | collective-permute-start | bytes 3538952 | tf_op jit(solution)/shard_map/ppermute | solution.py:21
  12.7 1.9 %collective-permute-start.2 = (f32[2,192,768]{2,1,0:T(8,128)}, f32[2,192,768]{2,1,0:T(8,128)S(1)}, u32[]{:S(2)}, u32[]{:S(2)}) collective-permute-start(f32[2,192,768]{2,1,0:T(8,128)} %psi.1), channel_id=1, source_target_pairs={{0,1},{1,0},{2,3},{3,2},{4,5},{5,4},{6,7},{7,6},{8,9},{9,8},{10,11... | collective-permute-start | bytes 3538952 | tf_op jit(solution)/shard_map/ppermute | solution.py:21
  14.6 2.4 %collective-permute-start.5 = (f32[2,192,768]{2,1,0:T(8,128)}, f32[2,192,768]{2,1,0:T(8,128)}, u32[]{:S(2)}, u32[]{:S(2)}) collective-permute-start(f32[2,192,768]{2,1,0:T(8,128)} %right.1), channel_id=1, source_target_pairs={{0,1},{1,0},{2,3},{3,2},{4,5},{5,4},{6,7},{7,6},{8,9},{9,8},{10,11... | collective-permute-start | bytes 3538952 | tf_op jit(solution)/shard_map/ppermute | solution.py:21
  17.0 13.7 %collective-permute-done.3.psi_z = f32[2,192,768]{2,1,0:T(8,128)} collective-permute-done((f32[2,192,768]{2,1,0:T(8,128)}, f32[2,192,768]{2,1,0:T(8,128)}, u32[]{:S(2)}, u32[]{:S(2)}) %collective-permute-start.3) | collective-permute-done | bytes 1179680 | tf_op jit(solution)/shard_map/ppermute | solution.py:26
  30.7 1.9 %collective-permute-start.4 = (f32[2,192,768]{2,1,0:T(8,128)}, f32[2,192,768]{2,1,0:T(8,128)}, u32[]{:S(2)}, u32[]{:S(2)}) collective-permute-start(f32[2,192,768]{2,1,0:T(8,128)} %collective-permute-done.3.psi_z), channel_id=1, source_target_pairs={{0,1},{1,0},{2,3},{3,2},{4,5},{5,4},{6,7},{7,6},{8,9},{9,8},{10,11... | collective-permute-start | bytes 3538952 | tf_op jit(solution)/shard_map/ppermute | solution.py:21
  32.6 6.0 %collective-permute-done.6.right_z = f32[2,192,768]{2,1,0:T(8,128)} collective-permute-done((f32[2,192,768]{2,1,0:T(8,128)}, f32[2,192,768]{2,1,0:T(8,128)}, u32[]{:S(2)}, u32[]{:S(2)}) %collective-permute-start.6) | collective-permute-done | bytes 1179680 | tf_op jit(solution)/shard_map/ppermute | solution.py:21
  38.6 1.9 %collective-permute-start.7 = (f32[2,192,768]{2,1,0:T(8,128)}, f32[2,192,768]{2,1,0:T(8,128)}, u32[]{:S(2)}, u32[]{:S(2)}) collective-permute-start(f32[2,192,768]{2,1,0:T(8,128)} %collective-permute-done.6.right_z), channel_id=1, source_target_pairs={{0,1},{1,0},{2,3},{3,2},{4,5},{5,4},{6,7},{7,6},{8,9},{9,8},{10,11... | collective-permute-start | bytes 3538952 | tf_op jit(solution)/shard_map/ppermute | solution.py:21
  40.6 7.7 %collective-permute-start.1 = (f32[192,768]{1,0:T(8,128)}, f32[192,768]{1,0:T(8,128)S(1)}, u32[]{:S(2)}, u32[]{:S(2)}) collective-permute-start(f32[192,768]{1,0:T(8,128)} %bitcast.8), channel_id=1, source_target_pairs={{0,256},{128,384},{256,0},{384,128},{1,257},{129,385},{257,1},{385... | collective-permute-start | bytes 1769480 | tf_op jit(solution)/shard_map/ppermute | solution.py:21
  48.3 0.1 pad_add_fusion.place
  49.0 0.7 compare_select_fusion
  49.7 0.7 iota_compare_fusion
  50.4 0.1 fusion
  50.5 1.5 %shard_map.75 = (bf16[2,192,768]{2,1,0:T(8,128)(2,1)S(1)}, bf16[2,192,768]{2,1,0:T(8,128)(2,1)S(1)}) custom-call(f32[2,192,768]{2,1,0:T(8,128)} %collective-permute-done.3.psi_z), custom_call_target="tpu_custom_call" | custom-call | flops 1048576 | bytes 8388608 | tf_op jit(solution)/shard_map/pallas_call | solution.py:162
  51.9 0.0 copy-start.1
  52.0 0.0 collective-permute-done.2.psi_c
  52.0 2.1 %collective-permute-start = (f32[2,2]{1,0:T(2,128)S(1)}, f32[2,2]{1,0:T(2,128)S(1)}, u32[]{:S(2)}, u32[]{:S(2)}) collective-permute-start(f32[2,2]{1,0:T(2,128)S(1)} %fusion), channel_id=1, source_target_pairs={{0,256},{128,384},{256,0},{384,128},{1,257},{129,385},{257,1},{385... | collective-permute-start | bytes 56 | tf_op jit(solution)/shard_map/ppermute | solution.py:21
  54.1 0.0 copy-done
  54.1 1.0 shard_map.73
  55.1 19.5 %collective-permute-done.mix = f32[2,2]{1,0:T(2,128)S(1)} collective-permute-done((f32[2,2]{1,0:T(2,128)S(1)}, f32[2,2]{1,0:T(2,128)S(1)}, u32[]{:S(2)}, u32[]{:S(2)}) %collective-permute-start) | collective-permute-done | bytes 48 | tf_op jit(solution)/shard_map/ppermute | solution.py:21
  74.6 0.0 collective-permute-done.5.right_c
  74.6 0.0 copy-done.1
  74.6 1.8 %shard_map.77 = (bf16[2,2,192,768]{3,2,1,0:T(8,128)(2,1)S(1)}, bf16[2,2,192,768]{3,2,1,0:T(8,128)(2,1)S(1)}) custom-call(f32[2,2]{1,0:T(2,128)S(1)} %collective-permute-done.mix, f32[2,192,768]{2,1,0:T(8,128)S(1)} %copy-done.1, f32[2,192,768]{2,1,0:T(8,128)} %collective-permute-done.5.right_c), custom_call_target="tpu_custom_call" | custom-call | flops 1048576 | bytes 8388608 | tf_op jit(solution)/shard_map/pallas_call | solution.py:155
  76.4 0.0 collective-permute-done.1.left
  76.4 1.6 %shard_map.74.near = f32[2,192,768]{2,1,0:T(8,128)S(1)} custom-call(s32[2]{0:T(128)S(1)} %pad_add_fusion.place, f32[192,768]{1,0:T(8,128)S(1)} %collective-permute-done.1.left, bf16[2,384,768]{2,1,0:T(8,128)(2,1)S(1)} %get-tuple-element.13.psi_h, bf16[2,384,768]{2,1,0:T(8,128)(2,1)S(1)} %get-tuple-element.14.psi_l), custom_call_target="tpu_custom_call" | custom-call | flops 679477248 | bytes 8388608 | tf_op jit(solution)/shard_map/pallas_call | solution.py:158
  78.1 0.0 collective-permute-done.4.psi_zc
  78.1 2.5 %shard_map.76 = (bf16[2,192,768]{2,1,0:T(8,128)(2,1)S(1)}, bf16[2,192,768]{2,1,0:T(8,128)(2,1)S(1)}) custom-call(s32[2]{0:T(128)S(1)} %pad_add_fusion.place, f32[192,768]{1,0:T(8,128)S(1)} %collective-permute-done.1.left, f32[2,192,768]{2,1,0:T(8,128)S(1)} %shard_map.74.near, bf16[2,192,768]{2,1,0:T(8,128)(2,1)S(1)} %get-tuple-element.15.next_h, ...), custom_call_target="tpu_custom_call" | custom-call | flops 679477248 | bytes 8388608 | tf_op jit(solution)/shard_map/pallas_call | solution.py:163
  80.5 0.0 collective-permute-done.7.right_zc
  80.5 3.9 %shard_map.78 = f32[8,4,24,384]{3,2,1,0:T(8,128)S(1)} custom-call(s32[2]{0:T(128)S(1)} %pad_add_fusion.place, f32[2,2]{1,0:T(2,128)S(1)} %collective-permute-done.mix, bf16[2,192,768]{2,1,0:T(8,128)(2,1)S(1)} %get-tuple-element.17.inner_h, bf16[2,192,768]{2,1,0:T(8,128)(2,1)S(1)} %get-tuple-element.18.inner_l, ...), custom_call_target="tpu_custom_call" | custom-call | flops 1358954496 | bytes 8388608 | tf_op jit(solution)/shard_map/pallas_call | solution.py:169
  84.5 22.5 %all_to_all.10 = f32[8,96,384]{2,1,0:T(8,128)S(1)} all-to-all(f32[8,96,384]{2,1,0:T(8,128)S(1)} %bitcast.7), channel_id=1, replica_groups=mesh['yh'=4,'yl'=2,'zh'=4,'x'=4,'zl'=2,'c'=2] {'x','yl'}, dimensions={0} | all-to-all | bytes 2359296 | tf_op jit(solution)/shard_map/all_to_all | solution.py:181
  107.0 0.1 reduce_sum.28
  107.1 21.2 %all_to_all.11 = f32[16,6,384]{2,1,0:T(8,128)S(1)} all-to-all(f32[16,6,384]{2,1,0:T(8,128)S(1)} %reshape.48), channel_id=1, replica_groups=mesh['yh'=4,'yl'=2,'zh'=4,'x'=4,'zl'=2,'c'=2] {'yh','zh'}, dimensions={0} | all-to-all | bytes 294912 | tf_op jit(solution)/shard_map/all_to_all | solution.py:183
  128.4 0.7 reshape.49
  (2 shorter events, 0.0 us)
Async XLA Ops:
  0.0 54.1 %copy-start = (f32[2,192,768]{2,1,0:T(8,128)S(1)}, f32[2,192,768]{2,1,0:T(8,128)}, u32[]{:S(2)}) copy-start(f32[2,192,768]{2,1,0:T(8,128)} %psi.1) | copy-start | bytes 3538948
  0.0 30.7 %collective-permute-start.3 = (f32[2,192,768]{2,1,0:T(8,128)}, f32[2,192,768]{2,1,0:T(8,128)}, u32[]{:S(2)}, u32[]{:S(2)}) collective-permute-start(f32[2,192,768]{2,1,0:T(8,128)} %psi.1), channel_id=1, source_target_pairs={{0,50},{2,16},{16,2},{18,32},{32,18},{34,48},{48,34},{50,0},{1,51}... | collective-permute-start | bytes 3538952 | tf_op jit(solution)/shard_map/ppermute | solution.py:26
  4.4 34.2 %collective-permute-start.6 = (f32[2,192,768]{2,1,0:T(8,128)}, f32[2,192,768]{2,1,0:T(8,128)}, u32[]{:S(2)}, u32[]{:S(2)}) collective-permute-start(f32[2,192,768]{2,1,0:T(8,128)} %right.1), channel_id=1, source_target_pairs={{0,2},{2,0},{1,3},{3,1},{4,6},{6,4},{5,7},{7,5},{8,10},{10,8},{9,1... | collective-permute-start | bytes 3538952 | tf_op jit(solution)/shard_map/ppermute | solution.py:21
  12.7 39.3 %collective-permute-start.2 = (f32[2,192,768]{2,1,0:T(8,128)}, f32[2,192,768]{2,1,0:T(8,128)S(1)}, u32[]{:S(2)}, u32[]{:S(2)}) collective-permute-start(f32[2,192,768]{2,1,0:T(8,128)} %psi.1), channel_id=1, source_target_pairs={{0,1},{1,0},{2,3},{3,2},{4,5},{5,4},{6,7},{7,6},{8,9},{9,8},{10,11... | collective-permute-start | bytes 3538952 | tf_op jit(solution)/shard_map/ppermute | solution.py:21
  14.6 60.0 %collective-permute-start.5 = (f32[2,192,768]{2,1,0:T(8,128)}, f32[2,192,768]{2,1,0:T(8,128)}, u32[]{:S(2)}, u32[]{:S(2)}) collective-permute-start(f32[2,192,768]{2,1,0:T(8,128)} %right.1), channel_id=1, source_target_pairs={{0,1},{1,0},{2,3},{3,2},{4,5},{5,4},{6,7},{7,6},{8,9},{9,8},{10,11... | collective-permute-start | bytes 3538952 | tf_op jit(solution)/shard_map/ppermute | solution.py:21
  30.7 47.4 %collective-permute-start.4 = (f32[2,192,768]{2,1,0:T(8,128)}, f32[2,192,768]{2,1,0:T(8,128)}, u32[]{:S(2)}, u32[]{:S(2)}) collective-permute-start(f32[2,192,768]{2,1,0:T(8,128)} %collective-permute-done.3.psi_z), channel_id=1, source_target_pairs={{0,1},{1,0},{2,3},{3,2},{4,5},{5,4},{6,7},{7,6},{8,9},{9,8},{10,11... | collective-permute-start | bytes 3538952 | tf_op jit(solution)/shard_map/ppermute | solution.py:21
  38.6 41.9 %collective-permute-start.7 = (f32[2,192,768]{2,1,0:T(8,128)}, f32[2,192,768]{2,1,0:T(8,128)}, u32[]{:S(2)}, u32[]{:S(2)}) collective-permute-start(f32[2,192,768]{2,1,0:T(8,128)} %collective-permute-done.6.right_z), channel_id=1, source_target_pairs={{0,1},{1,0},{2,3},{3,2},{4,5},{5,4},{6,7},{7,6},{8,9},{9,8},{10,11... | collective-permute-start | bytes 3538952 | tf_op jit(solution)/shard_map/ppermute | solution.py:21
  40.6 35.9 %collective-permute-start.1 = (f32[192,768]{1,0:T(8,128)}, f32[192,768]{1,0:T(8,128)S(1)}, u32[]{:S(2)}, u32[]{:S(2)}) collective-permute-start(f32[192,768]{1,0:T(8,128)} %bitcast.8), channel_id=1, source_target_pairs={{0,256},{128,384},{256,0},{384,128},{1,257},{129,385},{257,1},{385... | collective-permute-start | bytes 1769480 | tf_op jit(solution)/shard_map/ppermute | solution.py:21
  51.9 22.7 %copy-start.1 = (f32[2,192,768]{2,1,0:T(8,128)S(1)}, f32[2,192,768]{2,1,0:T(8,128)}, u32[]{:S(2)}) copy-start(f32[2,192,768]{2,1,0:T(8,128)} %right.1) | copy-start | bytes 3538948
  52.0 22.6 %collective-permute-start = (f32[2,2]{1,0:T(2,128)S(1)}, f32[2,2]{1,0:T(2,128)S(1)}, u32[]{:S(2)}, u32[]{:S(2)}) collective-permute-start(f32[2,2]{1,0:T(2,128)S(1)} %fusion), channel_id=1, source_target_pairs={{0,256},{128,384},{256,0},{384,128},{1,257},{129,385},{257,1},{385... | collective-permute-start | bytes 56 | tf_op jit(solution)/shard_map/ppermute | solution.py:21

commit v3 on v2

--- a/solution.py
+++ b/solution.py
@@ -14,6 +14,7 @@
 VMEM = pl.BlockSpec(memory_space=pltpu.VMEM)
 SMEM = pl.BlockSpec(memory_space=pltpu.SMEM)
 MIB = 1 << 20
+GROUPS = ((3, 0), (1, 2))
 
 
 def shifted(block, axis, distance):
@@ -57,12 +58,6 @@
             psi_h[s, at, :], psi_l[s, at, :] = halves(p[s])
 
 
-def mix_kernel(mix, right, right_c, comb_h, comb_l):
-    for i, r in enumerate((right, right_c)):
-        for s in range(comb_h.shape[1]):
-            comb_h[i, s], comb_l[i, s] = halves(mixed(mix, r, s))
-
-
 def near_kernel(place, left, psi_h, psi_l, near):
     half = psi_h.shape[1]
     mine = halves(left[:, pl.ds(pl.multiple_of(place[0] * half, 128), half)])
@@ -88,27 +83,34 @@
         inner_h[s], inner_l[s] = halves(inner)
 
 
-def term_kernel(place, mix, inner_h, inner_l, comb_h, comb_l, right_z, right_zc, out, part, held, sem):
-    sectors, _, _ = inner_h.shape
+def term_kernel(place, mix, inner_h, inner_l, right, right_c, right_z, right_zc, out, part, held, sems):
+    sectors, rows, _ = inner_h.shape
     mine = place[0] * 2 + place[1]
-    fetch = pltpu.make_async_copy(right_z, held, sem)
-    fetch.start()
-    for i in range(4):
-        if i == 2:
-            fetch.wait()
+    fetches = [
+        pltpu.make_async_copy(block, held.at[i], sems.at[i])
+        for i, block in enumerate((right, right_c, right_z))
+    ]
+    for fetch in fetches:
+        fetch.start()
+    for group in GROUPS:
+        blocks = []
+        for i in group:
+            if i < 3:
+                fetches[i].wait()
+            blocks.append(right_zc if i == 3 else held.at[i])
         both = []
         for s in range(sectors):
-            if i < 2:
-                comb = comb_h[i, s], comb_l[i, s]
-            else:
-                comb = halves(mixed(mix, held if i == 2 else right_zc, s))
+            parts = [halves(mixed(mix, block, s)) for block in blocks]
+            comb = [jnp.concatenate(p, axis=0) for p in zip(*parts)]
             both.append(three_pass(comb, (inner_h[s], inner_l[s]), TURNED))
-        part[...] = jnp.concatenate(both, axis=1)
-        for yl in range(2):
-            for zh in range(4):
-                for x in range(4):
-                    at = yl * 96 + zh * 24 + x * 6
-                    out[x * 2 + yl, mine ^ i, zh * 6 : zh * 6 + 6, :] = part[at : at + 6, :]
+        for n, i in enumerate(group):
+            rows_at = slice(n * rows, (n + 1) * rows)
+            part[i] = jnp.concatenate([b[rows_at] for b in both], axis=1)
+            for yl in range(2):
+                for zh in range(4):
+                    for x in range(4):
+                        at = yl * 96 + zh * 24 + x * 6
+                        out[x * 2 + yl, mine ^ i, zh * 6 : zh * 6 + 6, :] = part[i, at : at + 6, :]
 
 
 def call(kernel, shapes, specs, flops, scratch=()):
@@ -148,12 +150,8 @@
     place = jnp.stack([lax.axis_index("zl"), lax.axis_index("c")]).astype(jnp.int32)
     product_flops = 2 * sectors * rows * m * m
     prepared = shape((sectors, 2 * rows, m), bf16)
-    combined = shape((2, sectors, rows, m), bf16)
     psi_h, psi_l = call(split_kernel, (prepared, prepared), [SMEM] + [VMEM] * 2, MIB)(
         place, psi, psi_c
-    )
-    comb_h, comb_l = call(mix_kernel, (combined, combined), [SMEM] + [VMEM] * 2, MIB)(
-        mixing, right_ops, right_c
     )
     near = call(near_kernel, shape((sectors, rows, m), f32), [SMEM] + [VMEM] * 3, 3 * product_flops // 2)(
         place, left, psi_h, psi_l
@@ -169,14 +167,14 @@
     tall = call(
         term_kernel,
         shape((8, 4, 24, sectors * rows), f32),
-        [SMEM, SMEM] + [VMEM] * 4 + [pl.BlockSpec(memory_space=pl.ANY), VMEM],
+        [SMEM, SMEM, VMEM, VMEM] + [pl.BlockSpec(memory_space=pl.ANY)] * 3 + [VMEM],
         3 * product_flops,
         [
-            pltpu.VMEM((rows, sectors * rows), f32),
-            pltpu.VMEM((rights, rows, m), f32),
-            pltpu.SemaphoreType.DMA,
+            pltpu.VMEM((4, rows, sectors * rows), f32),
+            pltpu.VMEM((3, rights, rows, m), f32),
+            pltpu.SemaphoreType.DMA((3,)),
         ],
-    )(place, mixing, inner_h, inner_l, comb_h, comb_l, right_z, right_zc)
+    )(place, mixing, inner_h, inner_l, right_ops, right_c, right_z, right_zc)
 
     got = lax.all_to_all(tall.reshape(8, -1, sectors * rows), ("x", "yl"), 0, 0, tiled=True)
     small = got.sum(axis=0).reshape(16, -1, sectors * rows)

time: 130 us -> 131 us (level)
  the two profiles are of different devices: /device:TPU:64 before, /device:TPU:8 now
where the time goes in v3:
time: 131 us; the launch traced here: 130 us
  blocking collectives  42.8 us (33%)
  waiting for transfers between devices  42.4 us (32%)
  starting transfers between devices  30.9 us (24%)
  Pallas kernels  11.2 us (9%)
  other arithmetic  1.6 us (1%)
    ppermute x1, waiting for transfers between devices, from_next_pair(): lax.ppermute(block, ('zh', 'zl'), [(z, (z + (1 if z % 2 else -1)) % n) fo...  22.4 us
    all_to_all x1, blocking collectives, per_device(): own = lax.all_to_all(small, ('yh', 'zh'), 0, 0, tiled=True).sum(axis=0)  21.5 us
    all_to_all x1, blocking collectives, per_device(): lax.all_to_all(tall.reshape(8, -1, sectors * rows), ('x', 'yl'), 0, 0, ti...  21.3 us
    ppermute x7, waiting for transfers between devices, shifted(): lax.ppermute(block, axis, [(i, (i + distance) % n) for i in range(n)])  20 us
    ppermute x7, starting transfers between devices, shifted(): lax.ppermute(block, axis, [(i, (i + distance) % n) for i in range(n)])  19.8 us
    ppermute x1, starting transfers between devices, from_next_pair(): lax.ppermute(block, ('zh', 'zl'), [(z, (z + (1 if z % 2 else -1)) % n) fo...  11.1 us
    pallas_call x1, Pallas kernels, per_device(): call(term_kernel, shape((8, 4, 24, sectors * rows), f32), [SMEM, SMEM, VM...  4.56 us
  transfers between devices with their start and end apart: 8, of which 2 were waited for; matrix products, arithmetic and copies ran while one was open for 1% of the time, Pallas kernels for 5%

profile of v3, /device:TPU:8, one launch (start us, length us, event | category | flops | bytes accessed | tf_op | source)
XLA Modules:
  0.0 130.5 jit_solution(7104068674541956997)
XLA Ops:
  0.0 0.0 copy-start
  0.0 11.1 %collective-permute-start.3 = (f32[2,192,768]{2,1,0:T(8,128)}, f32[2,192,768]{2,1,0:T(8,128)}, u32[]{:S(2)}, u32[]{:S(2)}) collective-permute-start(f32[2,192,768]{2,1,0:T(8,128)} %psi.1), channel_id=1, source_target_pairs={{0,50},{2,16},{16,2},{18,32},{32,18},{34,48},{48,34},{50,0},{1,51}... | collective-permute-start | bytes 3538952 | tf_op jit(solution)/shard_map/ppermute | solution.py:27
  11.1 1.9 %collective-permute-start.6 = (f32[2,192,768]{2,1,0:T(8,128)}, f32[2,192,768]{2,1,0:T(8,128)}, u32[]{:S(2)}, u32[]{:S(2)}) collective-permute-start(f32[2,192,768]{2,1,0:T(8,128)} %right.1), channel_id=1, source_target_pairs={{0,2},{2,0},{1,3},{3,1},{4,6},{6,4},{5,7},{7,5},{8,10},{10,8},{9,1... | collective-permute-start | bytes 3538952 | tf_op jit(solution)/shard_map/ppermute | solution.py:22
  13.0 1.9 %collective-permute-start.2 = (f32[2,192,768]{2,1,0:T(8,128)}, f32[2,192,768]{2,1,0:T(8,128)S(1)}, u32[]{:S(2)}, u32[]{:S(2)}) collective-permute-start(f32[2,192,768]{2,1,0:T(8,128)} %psi.1), channel_id=1, source_target_pairs={{0,1},{1,0},{2,3},{3,2},{4,5},{5,4},{6,7},{7,6},{8,9},{9,8},{10,11... | collective-permute-start | bytes 3538952 | tf_op jit(solution)/shard_map/ppermute | solution.py:22
  14.9 22.4 %collective-permute-done.3.psi_z = f32[2,192,768]{2,1,0:T(8,128)} collective-permute-done((f32[2,192,768]{2,1,0:T(8,128)}, f32[2,192,768]{2,1,0:T(8,128)}, u32[]{:S(2)}, u32[]{:S(2)}) %collective-permute-start.3) | collective-permute-done | bytes 1179680 | tf_op jit(solution)/shard_map/ppermute | solution.py:27
  37.3 1.9 %collective-permute-start.4 = (f32[2,192,768]{2,1,0:T(8,128)}, f32[2,192,768]{2,1,0:T(8,128)}, u32[]{:S(2)}, u32[]{:S(2)}) collective-permute-start(f32[2,192,768]{2,1,0:T(8,128)} %collective-permute-done.3.psi_z), channel_id=1, source_target_pairs={{0,1},{1,0},{2,3},{3,2},{4,5},{5,4},{6,7},{7,6},{8,9},{9,8},{10,11... | collective-permute-start | bytes 3538952 | tf_op jit(solution)/shard_map/ppermute | solution.py:22
  39.3 2.4 %collective-permute-start.5 = (f32[2,192,768]{2,1,0:T(8,128)}, f32[2,192,768]{2,1,0:T(8,128)}, u32[]{:S(2)}, u32[]{:S(2)}) collective-permute-start(f32[2,192,768]{2,1,0:T(8,128)} %right.1), channel_id=1, source_target_pairs={{0,1},{1,0},{2,3},{3,2},{4,5},{5,4},{6,7},{7,6},{8,9},{9,8},{10,11... | collective-permute-start | bytes 3538952 | tf_op jit(solution)/shard_map/ppermute | solution.py:22
  41.7 0.0 collective-permute-done.6.right_z
  41.7 1.9 %collective-permute-start.7 = (f32[2,192,768]{2,1,0:T(8,128)}, f32[2,192,768]{2,1,0:T(8,128)}, u32[]{:S(2)}, u32[]{:S(2)}) collective-permute-start(f32[2,192,768]{2,1,0:T(8,128)} %collective-permute-done.6.right_z), channel_id=1, source_target_pairs={{0,1},{1,0},{2,3},{3,2},{4,5},{5,4},{6,7},{7,6},{8,9},{9,8},{10,11... | collective-permute-start | bytes 3538952 | tf_op jit(solution)/shard_map/ppermute | solution.py:22
  43.6 6.8 %collective-permute-start.1 = (f32[192,768]{1,0:T(8,128)}, f32[192,768]{1,0:T(8,128)S(1)}, u32[]{:S(2)}, u32[]{:S(2)}) collective-permute-start(f32[192,768]{1,0:T(8,128)} %bitcast.8), channel_id=1, source_target_pairs={{0,256},{128,384},{256,0},{384,128},{1,257},{129,385},{257,1},{385... | collective-permute-start | bytes 1769480 | tf_op jit(solution)/shard_map/ppermute | solution.py:22
  50.5 0.1 pad_add_fusion.place
  51.2 0.7 compare_select_fusion
  51.9 0.7 iota_compare_fusion
  52.5 0.1 fusion
  52.6 1.5 %shard_map.75 = (bf16[2,192,768]{2,1,0:T(8,128)(2,1)S(1)}, bf16[2,192,768]{2,1,0:T(8,128)(2,1)S(1)}) custom-call(f32[2,192,768]{2,1,0:T(8,128)} %collective-permute-done.3.psi_z), custom_call_target="tpu_custom_call" | custom-call | flops 1048576 | bytes 8388608 | tf_op jit(solution)/shard_map/pallas_call | solution.py:160
  54.1 0.0 collective-permute-done.2.psi_c
  54.1 2.9 %collective-permute-start = (f32[2,2]{1,0:T(2,128)S(1)}, f32[2,2]{1,0:T(2,128)S(1)}, u32[]{:S(2)}, u32[]{:S(2)}) collective-permute-start(f32[2,2]{1,0:T(2,128)S(1)} %fusion), channel_id=1, source_target_pairs={{0,256},{128,384},{256,0},{384,128},{1,257},{129,385},{257,1},{385... | collective-permute-start | bytes 56 | tf_op jit(solution)/shard_map/ppermute | solution.py:22
  57.0 0.0 copy-done
  57.1 1.0 shard_map.73
  58.0 20.0 %collective-permute-done.1.left = f32[192,768]{1,0:T(8,128)S(1)} collective-permute-done((f32[192,768]{1,0:T(8,128)}, f32[192,768]{1,0:T(8,128)S(1)}, u32[]{:S(2)}, u32[]{:S(2)}) %collective-permute-start.1) | collective-permute-done | bytes 589856 | tf_op jit(solution)/shard_map/ppermute | solution.py:22
  78.0 1.6 %shard_map.74.near = f32[2,192,768]{2,1,0:T(8,128)S(1)} custom-call(s32[2]{0:T(128)S(1)} %pad_add_fusion.place, f32[192,768]{1,0:T(8,128)S(1)} %collective-permute-done.1.left, bf16[2,384,768]{2,1,0:T(8,128)(2,1)S(1)} %get-tuple-element.11.psi_h, bf16[2,384,768]{2,1,0:T(8,128)(2,1)S(1)} %get-tuple-element.12.psi_l), custom_call_target="tpu_custom_call" | custom-call | flops 679477248 | bytes 8388608 | tf_op jit(solution)/shard_map/pallas_call | solution.py:156
  79.6 0.0 collective-permute-done.4.psi_zc
  79.7 0.0 copy-start.1
  79.7 2.6 %shard_map.76 = (bf16[2,192,768]{2,1,0:T(8,128)(2,1)S(1)}, bf16[2,192,768]{2,1,0:T(8,128)(2,1)S(1)}) custom-call(s32[2]{0:T(128)S(1)} %pad_add_fusion.place, f32[192,768]{1,0:T(8,128)S(1)} %collective-permute-done.1.left, f32[2,192,768]{2,1,0:T(8,128)S(1)} %shard_map.74.near, bf16[2,192,768]{2,1,0:T(8,128)(2,1)S(1)} %get-tuple-element.13.next_h, ...), custom_call_target="tpu_custom_call" | custom-call | flops 679477248 | bytes 8388608 | tf_op jit(solution)/shard_map/pallas_call | solution.py:161
  82.2 0.0 collective-permute-done.mix
  82.2 0.0 collective-permute-done.5.right_c
  82.3 0.0 collective-permute-done.7.right_zc
  82.3 0.0 copy-done.1
  82.3 4.6 %shard_map.77 = f32[8,4,24,384]{3,2,1,0:T(8,128)S(1)} custom-call(s32[2]{0:T(128)S(1)} %pad_add_fusion.place, f32[2,2]{1,0:T(2,128)S(1)} %collective-permute-done.mix, bf16[2,192,768]{2,1,0:T(8,128)(2,1)S(1)} %get-tuple-element.15.inner_h, bf16[2,192,768]{2,1,0:T(8,128)(2,1)S(1)} %get-tuple-element.16.inner_l, f32[2,192,768]{2,1,0:T(8,128)S(1)} %copy-done.1, ...), custom_call_target="tpu_custom_call" | custom-call | flops 1358954496 | bytes 8388608 | tf_op jit(solution)/shard_map/pallas_call | solution.py:167
  86.8 21.3 %all_to_all.10 = f32[8,96,384]{2,1,0:T(8,128)S(1)} all-to-all(f32[8,96,384]{2,1,0:T(8,128)S(1)} %bitcast.7), channel_id=1, replica_groups=mesh['yh'=4,'yl'=2,'zh'=4,'x'=4,'zl'=2,'c'=2] {'x','yl'}, dimensions={0} | all-to-all | bytes 2359296 | tf_op jit(solution)/shard_map/all_to_all | solution.py:179
  108.1 0.1 reduce_sum.28
  108.2 21.5 %all_to_all.11 = f32[16,6,384]{2,1,0:T(8,128)S(1)} all-to-all(f32[16,6,384]{2,1,0:T(8,128)S(1)} %reshape.48), channel_id=1, replica_groups=mesh['yh'=4,'yl'=2,'zh'=4,'x'=4,'zl'=2,'c'=2] {'yh','zh'}, dimensions={0} | all-to-all | bytes 294912 | tf_op jit(solution)/shard_map/all_to_all | solution.py:181
  129.8 0.7 reshape.49
  (2 shorter events, 0.0 us)
Async XLA Ops:
  0.0 57.0 %copy-start = (f32[2,192,768]{2,1,0:T(8,128)S(1)}, f32[2,192,768]{2,1,0:T(8,128)}, u32[]{:S(2)}) copy-start(f32[2,192,768]{2,1,0:T(8,128)} %psi.1) | copy-start | bytes 3538948
  0.0 37.3 %collective-permute-start.3 = (f32[2,192,768]{2,1,0:T(8,128)}, f32[2,192,768]{2,1,0:T(8,128)}, u32[]{:S(2)}, u32[]{:S(2)}) collective-permute-start(f32[2,192,768]{2,1,0:T(8,128)} %psi.1), channel_id=1, source_target_pairs={{0,50},{2,16},{16,2},{18,32},{32,18},{34,48},{48,34},{50,0},{1,51}... | collective-permute-start | bytes 3538952 | tf_op jit(solution)/shard_map/ppermute | solution.py:27
  11.1 30.6 %collective-permute-start.6 = (f32[2,192,768]{2,1,0:T(8,128)}, f32[2,192,768]{2,1,0:T(8,128)}, u32[]{:S(2)}, u32[]{:S(2)}) collective-permute-start(f32[2,192,768]{2,1,0:T(8,128)} %right.1), channel_id=1, source_target_pairs={{0,2},{2,0},{1,3},{3,1},{4,6},{6,4},{5,7},{7,5},{8,10},{10,8},{9,1... | collective-permute-start | bytes 3538952 | tf_op jit(solution)/shard_map/ppermute | solution.py:22
  13.0 41.1 %collective-permute-start.2 = (f32[2,192,768]{2,1,0:T(8,128)}, f32[2,192,768]{2,1,0:T(8,128)S(1)}, u32[]{:S(2)}, u32[]{:S(2)}) collective-permute-start(f32[2,192,768]{2,1,0:T(8,128)} %psi.1), channel_id=1, source_target_pairs={{0,1},{1,0},{2,3},{3,2},{4,5},{5,4},{6,7},{7,6},{8,9},{9,8},{10,11... | collective-permute-start | bytes 3538952 | tf_op jit(solution)/shard_map/ppermute | solution.py:22
  37.3 42.3 %collective-permute-start.4 = (f32[2,192,768]{2,1,0:T(8,128)}, f32[2,192,768]{2,1,0:T(8,128)}, u32[]{:S(2)}, u32[]{:S(2)}) collective-permute-start(f32[2,192,768]{2,1,0:T(8,128)} %collective-permute-done.3.psi_z), channel_id=1, source_target_pairs={{0,1},{1,0},{2,3},{3,2},{4,5},{5,4},{6,7},{7,6},{8,9},{9,8},{10,11... | collective-permute-start | bytes 3538952 | tf_op jit(solution)/shard_map/ppermute | solution.py:22
  39.3 43.0 %collective-permute-start.5 = (f32[2,192,768]{2,1,0:T(8,128)}, f32[2,192,768]{2,1,0:T(8,128)}, u32[]{:S(2)}, u32[]{:S(2)}) collective-permute-start(f32[2,192,768]{2,1,0:T(8,128)} %right.1), channel_id=1, source_target_pairs={{0,1},{1,0},{2,3},{3,2},{4,5},{5,4},{6,7},{7,6},{8,9},{9,8},{10,11... | collective-permute-start | bytes 3538952 | tf_op jit(solution)/shard_map/ppermute | solution.py:22
  41.7 40.6 %collective-permute-start.7 = (f32[2,192,768]{2,1,0:T(8,128)}, f32[2,192,768]{2,1,0:T(8,128)}, u32[]{:S(2)}, u32[]{:S(2)}) collective-permute-start(f32[2,192,768]{2,1,0:T(8,128)} %collective-permute-done.6.right_z), channel_id=1, source_target_pairs={{0,1},{1,0},{2,3},{3,2},{4,5},{5,4},{6,7},{7,6},{8,9},{9,8},{10,11... | collective-permute-start | bytes 3538952 | tf_op jit(solution)/shard_map/ppermute | solution.py:22
  43.6 34.4 %collective-permute-start.1 = (f32[192,768]{1,0:T(8,128)}, f32[192,768]{1,0:T(8,128)S(1)}, u32[]{:S(2)}, u32[]{:S(2)}) collective-permute-start(f32[192,768]{1,0:T(8,128)} %bitcast.8), channel_id=1, source_target_pairs={{0,256},{128,384},{256,0},{384,128},{1,257},{129,385},{257,1},{385... | collective-permute-start | bytes 1769480 | tf_op jit(solution)/shard_map/ppermute | solution.py:22
  54.1 28.1 %collective-permute-start = (f32[2,2]{1,0:T(2,128)S(1)}, f32[2,2]{1,0:T(2,128)S(1)}, u32[]{:S(2)}, u32[]{:S(2)}) collective-permute-start(f32[2,2]{1,0:T(2,128)S(1)} %fusion), channel_id=1, source_target_pairs={{0,256},{128,384},{256,0},{384,128},{1,257},{129,385},{257,1},{385... | collective-permute-start | bytes 56 | tf_op jit(solution)/shard_map/ppermute | solution.py:22
  79.7 2.6 %copy-start.1 = (f32[2,192,768]{2,1,0:T(8,128)S(1)}, f32[2,192,768]{2,1,0:T(8,128)}, u32[]{:S(2)}) copy-start(f32[2,192,768]{2,1,0:T(8,128)} %right.1) | copy-start | bytes 3538948

commit v4 on v3

--- a/solution.py
+++ b/solution.py
@@ -58,29 +58,24 @@
             psi_h[s, at, :], psi_l[s, at, :] = halves(p[s])
 
 
-def near_kernel(place, left, psi_h, psi_l, near):
-    half = psi_h.shape[1]
-    mine = halves(left[:, pl.ds(pl.multiple_of(place[0] * half, 128), half)])
-    for s in range(psi_h.shape[0]):
-        near[s] = three_pass(mine, (psi_h[s], psi_l[s]), ROW)
-
-
 def next_kernel(psi_z, next_h, next_l):
     for s in range(psi_z.shape[0]):
         next_h[s], next_l[s] = halves(psi_z[s])
 
 
-def far_kernel(place, left, near, next_h, next_l, psi_zc, inner_h, inner_l):
-    sectors, rows, half = psi_zc.shape[0], psi_zc.shape[1], left.shape[1] // 2
+def inner_kernel(place, left, psi_h, psi_l, next_h, next_l, psi_zc, inner_h, inner_l):
+    sectors, rows, _ = psi_zc.shape
+    half = 2 * rows
+    mine = left[:, pl.ds(pl.multiple_of(place[0] * half, 128), half)]
     other = left[:, pl.ds(pl.multiple_of((1 - place[0]) * half, 128), half)]
     swapped = jnp.concatenate([other[:, rows:], other[:, :rows]], axis=1)
-    other = halves(jnp.where(place[1] == 1, swapped, other))
+    other = jnp.where(place[1] == 1, swapped, other)
+    columns = halves(jnp.concatenate([mine, other], axis=1))
     for s in range(sectors):
         zc_h, zc_l = halves(psi_zc[s])
-        far_h = jnp.concatenate([next_h[s], zc_h], axis=0)
-        far_l = jnp.concatenate([next_l[s], zc_l], axis=0)
-        inner = near[s] + three_pass(other, (far_h, far_l), ROW)
-        inner_h[s], inner_l[s] = halves(inner)
+        all_h = jnp.concatenate([psi_h[s], next_h[s], zc_h], axis=0)
+        all_l = jnp.concatenate([psi_l[s], next_l[s], zc_l], axis=0)
+        inner_h[s], inner_l[s] = halves(three_pass(columns, (all_h, all_l), ROW))
 
 
 def term_kernel(place, mix, inner_h, inner_l, right, right_c, right_z, right_zc, out, part, held, sems):
@@ -110,7 +105,7 @@
                 for zh in range(4):
                     for x in range(4):
                         at = yl * 96 + zh * 24 + x * 6
-                        out[x * 2 + yl, mine ^ i, zh * 6 : zh * 6 + 6, :] = part[i, at : at + 6, :]
+                        out[yl * 4 + x, mine ^ i, zh * 6 : zh * 6 + 6, :] = part[i, at : at + 6, :]
 
 
 def call(kernel, shapes, specs, flops, scratch=()):
@@ -153,17 +148,11 @@
     psi_h, psi_l = call(split_kernel, (prepared, prepared), [SMEM] + [VMEM] * 2, MIB)(
         place, psi, psi_c
     )
-    near = call(near_kernel, shape((sectors, rows, m), f32), [SMEM] + [VMEM] * 3, 3 * product_flops // 2)(
-        place, left, psi_h, psi_l
-    )
     inner = shape((sectors, rows, m), bf16)
     next_h, next_l = call(next_kernel, (inner, inner), [VMEM], MIB)(psi_z)
     inner_h, inner_l = call(
-        far_kernel,
-        (inner, inner),
-        [SMEM] + [VMEM] * 5,
-        3 * product_flops // 2,
-    )(place, left, near, next_h, next_l, psi_zc)
+        inner_kernel, (inner, inner), [SMEM] + [VMEM] * 6, 3 * product_flops
+    )(place, left, psi_h, psi_l, next_h, next_l, psi_zc)
     tall = call(
         term_kernel,
         shape((8, 4, 24, sectors * rows), f32),
@@ -176,7 +165,7 @@
         ],
     )(place, mixing, inner_h, inner_l, right_ops, right_c, right_z, right_zc)
 
-    got = lax.all_to_all(tall.reshape(8, -1, sectors * rows), ("x", "yl"), 0, 0, tiled=True)
+    got = lax.all_to_all(tall.reshape(8, -1, sectors * rows), ("yl", "x"), 0, 0, tiled=True)
     small = got.sum(axis=0).reshape(16, -1, sectors * rows)
     own = lax.all_to_all(small, ("yh", "zh"), 0, 0, tiled=True).sum(axis=0)
     return own.reshape(-1, sectors, rows).transpose(1, 2, 0)

time: 131 us -> 130 us (level)
  the two profiles are of different devices: /device:TPU:8 before, /device:TPU:64 now
where the time goes in v4:
time: 130 us; the launch traced here: 129 us
  blocking collectives  46.2 us (36%)
  waiting for transfers between devices  40.6 us (31%)
  starting transfers between devices  30.5 us (23%)
  Pallas kernels  8.92 us (7%)
  other arithmetic  1.6 us (1%)
    ppermute x7, starting transfers between devices, shifted(): lax.ppermute(block, axis, [(i, (i + distance) % n) for i in range(n)])  26.1 us
    ppermute x7, waiting for transfers between devices, shifted(): lax.ppermute(block, axis, [(i, (i + distance) % n) for i in range(n)])  24.6 us
    all_to_all x1, blocking collectives, per_device(): own = lax.all_to_all(small, ('yh', 'zh'), 0, 0, tiled=True).sum(axis=0)  23.6 us
    all_to_all x1, blocking collectives, per_device(): lax.all_to_all(tall.reshape(8, -1, sectors * rows), ('yl', 'x'), 0, 0, ti...  22.6 us
    ppermute x1, waiting for transfers between devices, from_next_pair(): lax.ppermute(block, ('zh', 'zl'), [(z, (z + (1 if z % 2 else -1)) % n) fo...  16 us
    pallas_call x1, Pallas kernels, per_device(): call(term_kernel, shape((8, 4, 24, sectors * rows), f32), [SMEM, SMEM, VM...  4.57 us
    ppermute x1, starting transfers between devices, from_next_pair(): lax.ppermute(block, ('zh', 'zl'), [(z, (z + (1 if z % 2 else -1)) % n) fo...  4.4 us
    pallas_call x1, Pallas kernels, per_device(): call(inner_kernel, (inner, inner), [SMEM] + [VMEM] * 6, 3 * product_flops)  3.16 us
  transfers between devices with their start and end apart: 8, of which 3 were waited for; matrix products, arithmetic and copies ran while one was open for 1% of the time, Pallas kernels for 3%

profile of v4, /device:TPU:64, one launch (start us, length us, event | category | flops | bytes accessed | tf_op | source)
XLA Modules:
  0.0 129.4 jit_solution(4084303335887275031)
XLA Ops:
  0.0 0.0 copy-start
  0.0 4.4 %collective-permute-start.3 = (f32[2,192,768]{2,1,0:T(8,128)}, f32[2,192,768]{2,1,0:T(8,128)S(1)}, u32[]{:S(2)}, u32[]{:S(2)}) collective-permute-start(f32[2,192,768]{2,1,0:T(8,128)} %psi.1), channel_id=1, source_target_pairs={{0,50},{2,16},{16,2},{18,32},{32,18},{34,48},{48,34},{50,0},{1,51}... | collective-permute-start | bytes 3538952 | tf_op jit(solution)/shard_map/ppermute | solution.py:27
  4.4 8.2 %collective-permute-start.6 = (f32[2,192,768]{2,1,0:T(8,128)}, f32[2,192,768]{2,1,0:T(8,128)}, u32[]{:S(2)}, u32[]{:S(2)}) collective-permute-start(f32[2,192,768]{2,1,0:T(8,128)} %right.1), channel_id=1, source_target_pairs={{0,2},{2,0},{1,3},{3,1},{4,6},{6,4},{5,7},{7,5},{8,10},{10,8},{9,1... | collective-permute-start | bytes 3538952 | tf_op jit(solution)/shard_map/ppermute | solution.py:22
  12.7 1.9 %collective-permute-start.2 = (f32[2,192,768]{2,1,0:T(8,128)}, f32[2,192,768]{2,1,0:T(8,128)S(1)}, u32[]{:S(2)}, u32[]{:S(2)}) collective-permute-start(f32[2,192,768]{2,1,0:T(8,128)} %psi.1), channel_id=1, source_target_pairs={{0,1},{1,0},{2,3},{3,2},{4,5},{5,4},{6,7},{7,6},{8,9},{9,8},{10,11... | collective-permute-start | bytes 3538952 | tf_op jit(solution)/shard_map/ppermute | solution.py:22
  14.6 16.0 %collective-permute-done.3.psi_z = f32[2,192,768]{2,1,0:T(8,128)S(1)} collective-permute-done((f32[2,192,768]{2,1,0:T(8,128)}, f32[2,192,768]{2,1,0:T(8,128)S(1)}, u32[]{:S(2)}, u32[]{:S(2)}) %collective-permute-start.3) | collective-permute-done | bytes 1179680 | tf_op jit(solution)/shard_map/ppermute | solution.py:27
  30.6 1.9 %collective-permute-start.4 = (f32[2,192,768]{2,1,0:T(8,128)S(1)}, f32[2,192,768]{2,1,0:T(8,128)}, u32[]{:S(2)}, u32[]{:S(2)}) collective-permute-start(f32[2,192,768]{2,1,0:T(8,128)S(1)} %collective-permute-done.3.psi_z), channel_id=1, source_target_pairs={{0,1},{1,0},{2,3},{3,2},{4,5},{5,4},{6,7},{7,6},{8,9},{9,8},{10,11... | collective-permute-start | bytes 3538952 | tf_op jit(solution)/shard_map/ppermute | solution.py:22
  32.5 2.4 %collective-permute-start.5 = (f32[2,192,768]{2,1,0:T(8,128)}, f32[2,192,768]{2,1,0:T(8,128)}, u32[]{:S(2)}, u32[]{:S(2)}) collective-permute-start(f32[2,192,768]{2,1,0:T(8,128)} %right.1), channel_id=1, source_target_pairs={{0,1},{1,0},{2,3},{3,2},{4,5},{5,4},{6,7},{7,6},{8,9},{9,8},{10,11... | collective-permute-start | bytes 3538952 | tf_op jit(solution)/shard_map/ppermute | solution.py:22
  34.9 3.7 %collective-permute-done.6.right_z = f32[2,192,768]{2,1,0:T(8,128)} collective-permute-done((f32[2,192,768]{2,1,0:T(8,128)}, f32[2,192,768]{2,1,0:T(8,128)}, u32[]{:S(2)}, u32[]{:S(2)}) %collective-permute-start.6) | collective-permute-done | bytes 1179680 | tf_op jit(solution)/shard_map/ppermute | solution.py:22
  38.6 1.9 %collective-permute-start.7 = (f32[2,192,768]{2,1,0:T(8,128)}, f32[2,192,768]{2,1,0:T(8,128)}, u32[]{:S(2)}, u32[]{:S(2)}) collective-permute-start(f32[2,192,768]{2,1,0:T(8,128)} %collective-permute-done.6.right_z), channel_id=1, source_target_pairs={{0,1},{1,0},{2,3},{3,2},{4,5},{5,4},{6,7},{7,6},{8,9},{9,8},{10,11... | collective-permute-start | bytes 3538952 | tf_op jit(solution)/shard_map/ppermute | solution.py:22
  40.6 7.7 %collective-permute-start.1 = (f32[192,768]{1,0:T(8,128)}, f32[192,768]{1,0:T(8,128)}, u32[]{:S(2)}, u32[]{:S(2)}) collective-permute-start(f32[192,768]{1,0:T(8,128)} %bitcast.8), channel_id=1, source_target_pairs={{0,256},{128,384},{256,0},{384,128},{1,257},{129,385},{257,1},{385... | collective-permute-start | bytes 1769480 | tf_op jit(solution)/shard_map/ppermute | solution.py:22
  48.3 0.1 pad_add_fusion.place
  49.0 0.7 compare_select_fusion
  49.7 0.7 iota_compare_fusion
  50.4 0.1 fusion
  50.5 0.2 shard_map.74
  50.7 0.0 collective-permute-done.2.psi_c
  50.7 2.0 %collective-permute-start = (f32[2,2]{1,0:T(2,128)S(1)}, f32[2,2]{1,0:T(2,128)S(1)}, u32[]{:S(2)}, u32[]{:S(2)}) collective-permute-start(f32[2,2]{1,0:T(2,128)S(1)} %fusion), channel_id=1, source_target_pairs={{0,256},{128,384},{256,0},{384,128},{1,257},{129,385},{257,1},{385... | collective-permute-start | bytes 56 | tf_op jit(solution)/shard_map/ppermute | solution.py:22
  52.7 0.0 copy-done
  52.7 1.0 shard_map.73
  53.7 20.9 %collective-permute-done.1.left = f32[192,768]{1,0:T(8,128)} collective-permute-done((f32[192,768]{1,0:T(8,128)}, f32[192,768]{1,0:T(8,128)}, u32[]{:S(2)}, u32[]{:S(2)}) %collective-permute-start.1) | collective-permute-done | bytes 589856 | tf_op jit(solution)/shard_map/ppermute | solution.py:22
  74.6 0.0 collective-permute-done.4.psi_zc
  74.6 0.0 copy-start.1
  74.6 3.2 %shard_map.75 = (bf16[2,192,768]{2,1,0:T(8,128)(2,1)S(1)}, bf16[2,192,768]{2,1,0:T(8,128)(2,1)S(1)}) custom-call(s32[2]{0:T(128)S(1)} %pad_add_fusion.place, f32[192,768]{1,0:T(8,128)} %collective-permute-done.1.left, bf16[2,384,768]{2,1,0:T(8,128)(2,1)S(1)} %get-tuple-element.11.psi_h, bf16[2,384,768]{2,1,0:T(8,128)(2,1)S(1)} %get-tuple-element.12.psi_l, ...), custom_call_target="tpu_custom_call" | custom-call | flops 1358954496 | bytes 8388608 | tf_op jit(solution)/shard_map/pallas_call | solution.py:153
  77.8 0.0 collective-permute-done.mix
  77.8 0.0 collective-permute-done.5.right_c
  77.8 0.0 collective-permute-done.7.right_zc
  77.8 0.0 copy-done.1
  77.8 4.6 %shard_map.76 = f32[8,4,24,384]{3,2,1,0:T(8,128)S(1)} custom-call(s32[2]{0:T(128)S(1)} %pad_add_fusion.place, f32[2,2]{1,0:T(2,128)S(1)} %collective-permute-done.mix, bf16[2,192,768]{2,1,0:T(8,128)(2,1)S(1)} %get-tuple-element.15.inner_h, bf16[2,192,768]{2,1,0:T(8,128)(2,1)S(1)} %get-tuple-element.16.inner_l, f32[2,192,768]{2,1,0:T(8,128)S(1)} %copy-done.1, ...), custom_call_target="tpu_custom_call" | custom-call | flops 1358954496 | bytes 8388608 | tf_op jit(solution)/shard_map/pallas_call | solution.py:156
  82.4 22.6 %all_to_all.10 = f32[8,96,384]{2,1,0:T(8,128)S(1)} all-to-all(f32[8,96,384]{2,1,0:T(8,128)S(1)} %bitcast.7), channel_id=1, replica_groups=mesh['yh'=4,'yl'=2,'zh'=4,'x'=4,'zl'=2,'c'=2] {'yl','x'}, dimensions={0} | all-to-all | bytes 2359296 | tf_op jit(solution)/shard_map/all_to_all | solution.py:168
  105.0 0.1 reduce_sum.28
  105.1 23.6 %all_to_all.11 = f32[16,6,384]{2,1,0:T(8,128)S(1)} all-to-all(f32[16,6,384]{2,1,0:T(8,128)S(1)} %reshape.48), channel_id=1, replica_groups=mesh['yh'=4,'yl'=2,'zh'=4,'x'=4,'zl'=2,'c'=2] {'yh','zh'}, dimensions={0} | all-to-all | bytes 294912 | tf_op jit(solution)/shard_map/all_to_all | solution.py:170
  128.7 0.7 reshape.49
  (2 shorter events, 0.0 us)
Async XLA Ops:
  0.0 52.7 %copy-start = (f32[2,192,768]{2,1,0:T(8,128)S(1)}, f32[2,192,768]{2,1,0:T(8,128)}, u32[]{:S(2)}) copy-start(f32[2,192,768]{2,1,0:T(8,128)} %psi.1) | copy-start | bytes 3538948
  0.0 30.6 %collective-permute-start.3 = (f32[2,192,768]{2,1,0:T(8,128)}, f32[2,192,768]{2,1,0:T(8,128)S(1)}, u32[]{:S(2)}, u32[]{:S(2)}) collective-permute-start(f32[2,192,768]{2,1,0:T(8,128)} %psi.1), channel_id=1, source_target_pairs={{0,50},{2,16},{16,2},{18,32},{32,18},{34,48},{48,34},{50,0},{1,51}... | collective-permute-start | bytes 3538952 | tf_op jit(solution)/shard_map/ppermute | solution.py:27
  4.4 34.2 %collective-permute-start.6 = (f32[2,192,768]{2,1,0:T(8,128)}, f32[2,192,768]{2,1,0:T(8,128)}, u32[]{:S(2)}, u32[]{:S(2)}) collective-permute-start(f32[2,192,768]{2,1,0:T(8,128)} %right.1), channel_id=1, source_target_pairs={{0,2},{2,0},{1,3},{3,1},{4,6},{6,4},{5,7},{7,5},{8,10},{10,8},{9,1... | collective-permute-start | bytes 3538952 | tf_op jit(solution)/shard_map/ppermute | solution.py:22
  12.7 38.0 %collective-permute-start.2 = (f32[2,192,768]{2,1,0:T(8,128)}, f32[2,192,768]{2,1,0:T(8,128)S(1)}, u32[]{:S(2)}, u32[]{:S(2)}) collective-permute-start(f32[2,192,768]{2,1,0:T(8,128)} %psi.1), channel_id=1, source_target_pairs={{0,1},{1,0},{2,3},{3,2},{4,5},{5,4},{6,7},{7,6},{8,9},{9,8},{10,11... | collective-permute-start | bytes 3538952 | tf_op jit(solution)/shard_map/ppermute | solution.py:22
  30.6 44.0 %collective-permute-start.4 = (f32[2,192,768]{2,1,0:T(8,128)S(1)}, f32[2,192,768]{2,1,0:T(8,128)}, u32[]{:S(2)}, u32[]{:S(2)}) collective-permute-start(f32[2,192,768]{2,1,0:T(8,128)S(1)} %collective-permute-done.3.psi_z), channel_id=1, source_target_pairs={{0,1},{1,0},{2,3},{3,2},{4,5},{5,4},{6,7},{7,6},{8,9},{9,8},{10,11... | collective-permute-start | bytes 3538952 | tf_op jit(solution)/shard_map/ppermute | solution.py:22
  32.5 45.3 %collective-permute-start.5 = (f32[2,192,768]{2,1,0:T(8,128)}, f32[2,192,768]{2,1,0:T(8,128)}, u32[]{:S(2)}, u32[]{:S(2)}) collective-permute-start(f32[2,192,768]{2,1,0:T(8,128)} %right.1), channel_id=1, source_target_pairs={{0,1},{1,0},{2,3},{3,2},{4,5},{5,4},{6,7},{7,6},{8,9},{9,8},{10,11... | collective-permute-start | bytes 3538952 | tf_op jit(solution)/shard_map/ppermute | solution.py:22
  38.6 39.2 %collective-permute-start.7 = (f32[2,192,768]{2,1,0:T(8,128)}, f32[2,192,768]{2,1,0:T(8,128)}, u32[]{:S(2)}, u32[]{:S(2)}) collective-permute-start(f32[2,192,768]{2,1,0:T(8,128)} %collective-permute-done.6.right_z), channel_id=1, source_target_pairs={{0,1},{1,0},{2,3},{3,2},{4,5},{5,4},{6,7},{7,6},{8,9},{9,8},{10,11... | collective-permute-start | bytes 3538952 | tf_op jit(solution)/shard_map/ppermute | solution.py:22
  40.6 34.0 %collective-permute-start.1 = (f32[192,768]{1,0:T(8,128)}, f32[192,768]{1,0:T(8,128)}, u32[]{:S(2)}, u32[]{:S(2)}) collective-permute-start(f32[192,768]{1,0:T(8,128)} %bitcast.8), channel_id=1, source_target_pairs={{0,256},{128,384},{256,0},{384,128},{1,257},{129,385},{257,1},{385... | collective-permute-start | bytes 1769480 | tf_op jit(solution)/shard_map/ppermute | solution.py:22
  50.7 27.1 %collective-permute-start = (f32[2,2]{1,0:T(2,128)S(1)}, f32[2,2]{1,0:T(2,128)S(1)}, u32[]{:S(2)}, u32[]{:S(2)}) collective-permute-start(f32[2,2]{1,0:T(2,128)S(1)} %fusion), channel_id=1, source_target_pairs={{0,256},{128,384},{256,0},{384,128},{1,257},{129,385},{257,1},{385... | collective-permute-start | bytes 56 | tf_op jit(solution)/shard_map/ppermute | solution.py:22
  74.6 3.2 %copy-start.1 = (f32[2,192,768]{2,1,0:T(8,128)S(1)}, f32[2,192,768]{2,1,0:T(8,128)}, u32[]{:S(2)}) copy-start(f32[2,192,768]{2,1,0:T(8,128)} %right.1) | copy-start | bytes 3538948
